TPU v7x, 512 devices: a whole 4x8x8 slice. The times are simulated.
512 devices in a mesh: section: 16 (over y, core), ctx: 32 (over x, z).
Axes of the slice: x: 4, y: 8, z: 8, core: 2. Of those that a mesh axis runs over, the one named last changes fastest.
Arguments:
- query_rows: bfloat16 [65536, 4096], P(('section', 'ctx')), may hold values from -6 to 6
- key_rows: bfloat16 [65536, 4096], P(('section', 'ctx')), may hold values from -6 to 6
- value_rows: bfloat16 [65536, 4096], P(('section', 'ctx')), may hold values from -6 to 6
- short_taps: bfloat16 [16, 3, 3, 4096], P('section', None, None, 'ctx'), may hold values from -3 to 3
- long_taps: bfloat16 [16, 4096, 128], P('section', 'ctx'), may hold values from -0.5 to 0.5
- skip_gain: bfloat16 [16, 4096], P('section', 'ctx'), may hold values from 0.5 to 1.5
- prior_qkv: bfloat16 [16, 3, 2, 4096], P('section', None, None, 'ctx'), may hold values from -6 to 6
- prior_product: bfloat16 [16, 127, 4096], P('section', None, 'ctx'), may hold values from -6 to 6
Outputs:
- handed: bfloat16 [65536, 4096], P(('section', 'ctx'))
All inputs are finite; a program needn't handle non-finite values.
Results may differ from a plain program's by a relative error of at most 0.005.
Values may be sent and summed in bfloat16 or wider, within the bound.
No kernel may reach another device: no remote copies, remote signals or barrier semaphores. Data moves between devices by JAX's collectives and lax.ppermute only.
A program may use at most 128 MiB of HBM per device.

v0:
```python
import jax
import jax.numpy as jnp
from jax import lax
from jax.sharding import PartitionSpec as P


def passed_along(value, axis, steps):
    count = lax.axis_size(axis)
    pairs = [(source, (source + steps) % count) for source in range(count)]
    return lax.ppermute(value, axis, pairs)


def featurize(rows, history, taps):
    padded = jnp.concatenate([history, rows], axis=0).astype(jnp.float32)
    weights = taps.astype(jnp.float32)
    return weights[0] * padded[2:] + weights[1] * padded[1:-1] + weights[2] * padded[:-2]


def causal_filter(product, history, tap_rows):
    count, width = product.shape
    blocks = count // 128
    group = min(width, 128)
    groups = width // group
    padded = jnp.concatenate([jnp.zeros((1, width), product.dtype), history, product], axis=0)
    lower_rows = padded[:count].reshape(blocks, 128, groups, group).transpose(2, 0, 1, 3)
    upper_rows = padded[128:].reshape(blocks, 128, groups, group).transpose(2, 0, 1, 3)
    reversed_taps = tap_rows[:, ::-1]
    skewed = jnp.concatenate(
        [
            jnp.zeros((width, 1), tap_rows.dtype),
            reversed_taps,
            jnp.zeros((width, 128), tap_rows.dtype),
        ],
        axis=1,
    )
    skewed = skewed.reshape(groups, group, 257)

    def one_group(pieces):
        group_taps, lower_part, upper_part = pieces
        tiled = jnp.tile(group_taps, (1, 128))[:, : 128 * 256]
        toeplitz = tiled.reshape(group, 128, 256)
        own_part = jnp.einsum(
            "cij,bjc->bic", toeplitz[:, :, :128], lower_part, preferred_element_type=jnp.float32
        )
        prior_part = jnp.einsum(
            "cij,bjc->bic", toeplitz[:, :, 128:], upper_part, preferred_element_type=jnp.float32
        )
        return own_part + prior_part

    result = lax.map(one_group, (skewed, lower_rows, upper_rows))
    return result.transpose(1, 2, 0, 3).reshape(count, width)


def mixer(query_rows, key_rows, value_rows, edges, short_set, tap_rows, gain_row, send_tail):
    query_feat = featurize(query_rows, edges[0], short_set[0])
    key_feat = featurize(key_rows, edges[1], short_set[1])
    value_feat = featurize(value_rows, edges[2], short_set[2])
    product = (key_feat * value_feat).astype(jnp.bfloat16)
    history = send_tail(product)
    filtered = causal_filter(product, history, tap_rows)
    mixed = query_feat * (filtered + gain_row.astype(jnp.float32) * product.astype(jnp.float32))
    return mixed.astype(jnp.bfloat16)


def body(
    query_rows, key_rows, value_rows, short_taps, long_taps, skip_gain, prior_qkv, prior_product
):
    seq_query, seq_key, seq_value = (
        lax.all_to_all(query_rows, "ctx", split_axis=1, concat_axis=0, tiled=True),
        lax.all_to_all(key_rows, "ctx", split_axis=1, concat_axis=0, tiled=True),
        lax.all_to_all(value_rows, "ctx", split_axis=1, concat_axis=0, tiled=True),
    )
    own_prior = prior_qkv[0]

    def prior_tail(product):
        return prior_product[0]

    mixed = mixer(
        seq_query,
        seq_key,
        seq_value,
        (own_prior[0], own_prior[1], own_prior[2]),
        short_taps[0],
        long_taps[0],
        skip_gain[0],
        prior_tail,
    )
    rows_out = lax.all_to_all(mixed, "ctx", split_axis=0, concat_axis=1, tiled=True)
    return passed_along(rows_out, "section", 1)


def solution(mesh):
    in_specs = (
        P(("section", "ctx"), None),
        P(("section", "ctx"), None),
        P(("section", "ctx"), None),
        P("section", None, None, "ctx"),
        P("section", "ctx", None),
        P("section", "ctx"),
        P("section", None, None, "ctx"),
        P("section", None, "ctx"),
    )
    out_specs = P(("section", "ctx"), None)
    return jax.shard_map(body, mesh=mesh, in_specs=in_specs, out_specs=out_specs, check_vma=False)
```

profile of v0, /device:TPU:32, one launch (start us, length us, event | category | flops | bytes accessed | tf_op | source)
XLA Modules:
  0.0 184.4 jit_solution(714037403074118120)
XLA Ops:
  0.0 1.6 copy.41
  1.6 1.3 copy.42
  2.9 13.2 %all-to-all-start.1 = ((bf16[128,32,128]{2,0,1:T(8,128)(2,1)}), bf16[128,32,128]{2,0,1:T(8,128)(2,1)S(1)}, u32[]{:S(2)}, u32[]{:S(2)}) async-start(bf16[128,32,128]{2,0,1:T(8,128)(2,1)} %copy.42), calls=%async_computation.1 | async-start | bytes 2097152 | tf_op jit(solution)/shard_map/all_to_all | solution.py:70
  16.1 0.7 copy.45
  16.8 1.3 copy.46
  18.1 26.6 %all-to-all-done.1 = bf16[128,32,128]{2,0,1:T(8,128)(2,1)S(1)} async-done(((bf16[128,32,128]{2,0,1:T(8,128)(2,1)}), bf16[128,32,128]{2,0,1:T(8,128)(2,1)S(1)}, u32[]{:S(2)}, u32[]{:S(2)}) %all-to-all-start.1) | async-done | bytes 1048608 | tf_op jit(solution)/shard_map/all_to_all | solution.py:70
  44.8 5.1 %all-to-all-start.2 = ((bf16[128,32,128]{2,0,1:T(8,128)(2,1)}), bf16[128,32,128]{2,0,1:T(8,128)(2,1)S(1)}, u32[]{:S(2)}, u32[]{:S(2)}) async-start(bf16[128,32,128]{2,0,1:T(8,128)(2,1)} %copy.46), calls=%async_computation.2 | async-start | bytes 2097152 | tf_op jit(solution)/shard_map/all_to_all | solution.py:71
  50.3 4.5 %tile.14 = bf16[128,128,257]{0,2,1:T(8,128)(2,1)} broadcast(bf16[128,257]{0,1:T(8,128)(2,1)S(1)} %copy.50), dimensions={0,2} | broadcast | bytes 8487168 | tf_op jit(solution)/shard_map/while/body/eval_jaxpr/tile | solution.py:40
  54.7 12.9 %tile.15 = bf16[128,32896]{0,1:T(8,128)(2,1)} reshape(bf16[128,128,257]{0,2,1:T(8,128)(2,1)} %tile.14) | data formatting | bytes 16842752 | tf_op jit(solution)/shard_map/while/body/eval_jaxpr/tile | solution.py:40
  67.6 7.1 %slice.140 = bf16[128,32768]{0,1:T(8,128)(2,1)} slice(bf16[128,32896]{0,1:T(8,128)(2,1)} %tile.15), slice={[0:128], [0:32768]} | slice | bytes 16777216 | tf_op jit(solution)/shard_map/while/body/eval_jaxpr/slice | solution.py:40
  74.7 1.6 copy.37
  76.3 1.3 copy.38
  77.7 6.0 %fusion.10 = (bf16[128,128,128]{0,2,1:T(8,128)(2,1)}, bf16[128,128,128]{0,2,1:T(8,128)(2,1)}) fusion(bf16[128,128,256]{0,2,1:T(8,128)(2,1)} %bitcast.72), kind=kLoop, calls=%fused_computation.42 | loop fusion | bytes 16777216 | tf_op jit(solution)/shard_map/while/body/eval_jaxpr/slice | solution.py:46
  83.8 10.2 %all-to-all-start = ((bf16[128,32,128]{2,0,1:T(8,128)(2,1)}), bf16[128,32,128]{2,0,1:T(8,128)(2,1)}, u32[]{:S(2)}, u32[]{:S(2)}) async-start(bf16[128,32,128]{2,0,1:T(8,128)(2,1)} %copy.38), calls=%async_computation | async-start | bytes 2097152 | tf_op jit(solution)/shard_map/all_to_all | solution.py:69
  94.4 6.7 %copy.56 = bf16[128,128,128]{2,1,0:T(8,128)(2,1)} copy(bf16[128,128,128]{0,2,1:T(8,128)(2,1)} %get-tuple-element.14) | data formatting | bytes 8388608
  101.2 6.8 %copy.57 = bf16[128,128,128]{2,1,0:T(8,128)(2,1)} copy(bf16[128,128,128]{0,2,1:T(8,128)(2,1)} %get-tuple-element.13) | data formatting | bytes 8388608
  108.1 0.5 copy.44
  108.6 0.5 copy.48
  109.1 1.2 maximum_convert_fusion.1
  110.3 2.5 %fusion.4 = bf16[4096,128]{0,1:T(8,128)(2,1)S(1)} fusion(f32[4098,128]{0,1:T(8,128)S(1)} %get-tuple-element.41, f32[4098,128]{0,1:T(8,128)S(1)} %get-tuple-element.40, f32[128]{0:T(128)S(1)} %get-tuple-element.32, f32[128]{0:T(128)S(1)} %get-tuple-element.33, f32[128]{0:T(128)S(1)} %get-tuple-element.31, f32[128]{0:T(128)S(1)} %get-tuple-element.38, ...), kind=kLoop, calls=%fused_computation.6 | loop fusion | flops 6291456 | bytes 13634560 | tf_op jit(solution)/shard_map/convert_element_type | solution.py:58
  112.9 0.8 concatenate.18
  114.3 7.2 %all-to-all-done = bf16[128,32,128]{2,0,1:T(8,128)(2,1)} async-done(((bf16[128,32,128]{2,0,1:T(8,128)(2,1)}), bf16[128,32,128]{2,0,1:T(8,128)(2,1)}, u32[]{:S(2)}, u32[]{:S(2)}) %all-to-all-start) | async-done | bytes 1048608 | tf_op jit(solution)/shard_map/all_to_all | solution.py:69
  121.5 2.3 %copy.40 = bf16[4096,128]{0,1:T(8,128)(2,1)} copy(bf16[4096,128]{1,0:T(8,128)(2,1)} %bitcast.4) | data formatting | bytes 2097152 | tf_op jit(solution)/shard_map/all_to_all | solution.py:69
  123.8 4.6 %fusion.11 = f32[128,32,128]{2,1,0:T(8,128)S(1)} fusion(bf16[32,128,128]{1,0,2:T(8,128)(2,1)S(1)} %bitcast.76, bf16[128,128,128]{2,1,0:T(8,128)(2,1)} %copy.56), kind=kOutput, calls=%fused_computation.43 | convolution fusion | flops 134217728 | bytes 7340032 | tf_op jit(solution)/shard_map/while/body/eval_jaxpr/cij,bjc->bic/dot_general | solution.py:42
  128.4 0.4 maximum_convert_fusion
  128.8 2.3 %convolution_add_fusion = f32[128,32,128]{2,1,0:T(8,128)S(1)} fusion(f32[128,32,128]{2,1,0:T(8,128)S(1)} %fusion.11, bf16[32,128,128]{1,0,2:T(8,128)(2,1)S(1)} %bitcast.75, bf16[128,128,128]{2,1,0:T(8,128)(2,1)S(1)} %copy-done), kind=kOutput, calls=%fused_computation.20 | convolution fusion | flops 134742016 | bytes 9437184 | tf_op jit(solution)/shard_map/while/body/eval_jaxpr/cij,bjc->bic/dot_general | solution.py:45
  131.1 2.9 %fusion.1 = bf16[4096,128]{0,1:T(8,128)(2,1)S(1)} fusion(f32[16,8,32,128]{3,2,1,0:T(8,128)S(1)} %bitcast.74, f32[4098,128]{0,1:T(8,128)S(1)} %maximum_convert_fusion, bf16[4096,128]{0,1:T(8,128)(2,1)S(1)} %fusion.4, f32[128]{0:T(128)S(1)} %bitcast_convert_fusion, f32[128]{0:T(128)S(1)} %get-tuple-element.26, f32[128]{0:T(128)S(1)} %get-tuple-element.27, ...), kind=kLoop, calls=%fused_computation.2 | loop fusion | flops 5242880 | bytes 10487808 | tf_op jit(solution)/shard_map/convert_element_type | solution.py:62
  134.0 0.7 copy.52
  134.6 32.4 %all_to_all.76 = bf16[32,128,128]{2,1,0:T(8,128)(2,1)S(1)} all-to-all(bf16[32,128,128]{2,1,0:T(8,128)(2,1)S(1)} %bitcast.79), channel_id=1, replica_groups=mesh['section'=16,'ctx'=32] {'ctx'}, dimensions={0} | all-to-all | bytes 2097152 | tf_op jit(solution)/shard_map/all_to_all | solution.py:88
  167.0 0.7 copy.53
  167.7 15.4 %collective-permute-done = bf16[128,4096]{0,1:T(8,128)(2,1)S(1)} collective-permute-done((bf16[128,4096]{0,1:T(8,128)(2,1)S(1)}, bf16[128,4096]{0,1:T(8,128)(2,1)S(1)}, u32[]{:S(2)}, u32[]{:S(2)}) %collective-permute-start) | collective-permute-done | bytes 1048608 | tf_op jit(solution)/shard_map/ppermute | solution.py:10
  183.1 1.3 copy.54
  (37 shorter events, 1.6 us)
Async XLA Ops:
  1.6 14.5 %copy-start.2 = (bf16[128,4096]{1,0:T(8,128)(2,1)S(1)}, bf16[128,4096]{1,0:T(8,128)(2,1)}, u32[]{:S(2)}) copy-start(bf16[128,4096]{1,0:T(8,128)(2,1)} %param.10) | copy-start | bytes 3145732
  2.9 41.8 %all-to-all-start.1 = ((bf16[128,32,128]{2,0,1:T(8,128)(2,1)}), bf16[128,32,128]{2,0,1:T(8,128)(2,1)S(1)}, u32[]{:S(2)}, u32[]{:S(2)}) async-start(bf16[128,32,128]{2,0,1:T(8,128)(2,1)} %copy.42), calls=%async_computation.1 | async-start | bytes 2097152 | tf_op jit(solution)/shard_map/all_to_all | solution.py:70
  16.8 33.0 %copy-start.3 = (bf16[1,128,128]{2,1,0:T(8,128)(2,1)S(1)}, bf16[1,128,128]{2,1,0:T(8,128)(2,1)}, u32[]{:S(2)}) copy-start(bf16[1,128,128]{2,1,0:T(8,128)(2,1)} %param.12) | copy-start | bytes 98308
  44.8 39.0 %all-to-all-start.2 = ((bf16[128,32,128]{2,0,1:T(8,128)(2,1)}), bf16[128,32,128]{2,0,1:T(8,128)(2,1)S(1)}, u32[]{:S(2)}, u32[]{:S(2)}) async-start(bf16[128,32,128]{2,0,1:T(8,128)(2,1)} %copy.46), calls=%async_computation.2 | async-start | bytes 2097152 | tf_op jit(solution)/shard_map/all_to_all | solution.py:71
  74.7 3.0 %copy-start.6 = (bf16[1,3,2,128]{3,2,1,0:T(2,128)(2,1)S(1)}, bf16[1,3,2,128]{3,2,1,0:T(2,128)(2,1)}, u32[]{:S(2)}) copy-start(bf16[1,3,2,128]{3,2,1,0:T(2,128)(2,1)} %param.14) | copy-start | bytes 4612
  74.7 3.0 %copy-start.5 = (bf16[1,3,3,128]{3,2,1,0:T(4,128)(2,1)S(1)}, bf16[1,3,3,128]{3,2,1,0:T(4,128)(2,1)}, u32[]{:S(2)}) copy-start(bf16[1,3,3,128]{3,2,1,0:T(4,128)(2,1)} %param.11) | copy-start | bytes 6916
  83.8 10.3 %copy-start.7 = (bf16[1,128]{1,0:T(2,128)(2,1)S(1)}, bf16[1,128]{1,0:T(2,128)(2,1)}, u32[]{:S(2)}) copy-start(bf16[1,128]{1,0:T(2,128)(2,1)} %param.13) | copy-start | bytes 772
  83.8 10.5 %copy-start.4 = (bf16[1,127,128]{2,1,0:T(8,128)(2,1)S(1)}, bf16[1,127,128]{2,1,0:T(8,128)(2,1)}, u32[]{:S(2)}) copy-start(bf16[1,127,128]{2,1,0:T(8,128)(2,1)} %param.15) | copy-start | bytes 97540
  83.8 37.7 %all-to-all-start = ((bf16[128,32,128]{2,0,1:T(8,128)(2,1)}), bf16[128,32,128]{2,0,1:T(8,128)(2,1)}, u32[]{:S(2)}, u32[]{:S(2)}) async-start(bf16[128,32,128]{2,0,1:T(8,128)(2,1)} %copy.38), calls=%async_computation | async-start | bytes 2097152 | tf_op jit(solution)/shard_map/all_to_all | solution.py:69
  123.8 4.6 %copy-start.1 = (bf16[4096,128]{0,1:T(8,128)(2,1)S(1)}, bf16[4096,128]{0,1:T(8,128)(2,1)}, u32[]{:S(2)}) copy-start(bf16[4096,128]{0,1:T(8,128)(2,1)} %copy.40) | copy-start | bytes 3145732
  123.8 5.0 %copy-start = (bf16[128,128,128]{2,1,0:T(8,128)(2,1)S(1)}, bf16[128,128,128]{2,1,0:T(8,128)(2,1)}, u32[]{:S(2)}) copy-start(bf16[128,128,128]{2,1,0:T(8,128)(2,1)} %copy.57) | copy-start | bytes 12582916
  167.7 15.4 %collective-permute-start = (bf16[128,4096]{0,1:T(8,128)(2,1)S(1)}, bf16[128,4096]{0,1:T(8,128)(2,1)S(1)}, u32[]{:S(2)}, u32[]{:S(2)}) collective-permute-start(bf16[128,4096]{0,1:T(8,128)(2,1)S(1)} %bitcast.83), channel_id=1, source_target_pairs={{0,32},{32,64},{64,96},{96,128},{128,160},{160,192},{192,224},{224... | collective-permute-start | bytes 3145736 | tf_op jit(solution)/shard_map/ppermute | solution.py:10
where the time goes:
time: 186 us; the launch traced here: 184 us
  local copies, waits for them, and re-layouts  60 us (32%)
  waiting for transfers between devices  49.3 us (27%)
  blocking collectives  32.4 us (17%)
  starting transfers between devices  28.5 us (15%)
  other arithmetic  7.12 us (4%)
  matrix products  6.9 us (4%)
    all_to_all x1, blocking collectives, body(): lax.all_to_all(mixed, 'ctx', split_axis=0, concat_axis=1, tiled=True)  32.4 us
    all_to_all x1, waiting for transfers between devices, body(): lax.all_to_all(key_rows, 'ctx', split_axis=1, concat_axis=0, tiled=True)  26.6 us
    unnamed x24, local copies, waits for them, and re-layouts  18 us
    another operation x2, local copies, waits for them, and re-layouts, one_group(): tiled = jnp.tile(group_taps, (1, 128))[:, :128 * 256]  17.4 us
    ppermute x1, waiting for transfers between devices, passed_along(): return lax.ppermute(value, axis, pairs)  15.4 us
    all_to_all x1, starting transfers between devices, body(): lax.all_to_all(key_rows, 'ctx', split_axis=1, concat_axis=0, tiled=True)  13.2 us
    all_to_all x1, starting transfers between devices, body(): lax.all_to_all(query_rows, 'ctx', split_axis=1, concat_axis=0, tiled=True)  10.2 us
    all_to_all x1, waiting for transfers between devices, body(): lax.all_to_all(query_rows, 'ctx', split_axis=1, concat_axis=0, tiled=True)  7.21 us
  transfers between devices with their start and end apart: 4, of which 3 were waited for; matrix products, arithmetic and copies ran while one was open for 30% of the time, Pallas kernels for 0%

commit v1 on v0

v1 whole, which is shorter than its diff:
```python
import jax
import jax.numpy as jnp
import numpy as np
from jax import lax
from jax.experimental import pallas as pl
from jax.experimental.pallas import tpu as pltpu
from jax.sharding import Mesh
from jax.sharding import PartitionSpec as P

BF = jnp.bfloat16
F32 = jnp.float32
CHUNKS = 2
WIDTH = 512


def split_hi_lo(matrix):
    high = matrix.astype(np.float32).astype(BF)
    low = (matrix - high.astype(np.float64)).astype(np.float32).astype(BF)
    return high, low


def dft_matrices():
    n = np.arange(256, dtype=np.float64)[None, :]
    k = np.arange(128, dtype=np.float64)[:, None]
    angle = np.pi * (2 * k + 1) * n / 256
    forward = np.concatenate([np.cos(angle), np.sin(angle)], axis=0)
    inverse = forward.T[128:] / 128
    return split_hi_lo(forward), split_hi_lo(inverse)


def dot(a, b):
    return lax.dot_general(a, b, (((1,), (0,)), ((), ())), preferred_element_type=F32)


def dot_nt(a, b):
    return lax.dot_general(a, b, (((1,), (1,)), ((), ())), preferred_element_type=F32)


def featurize(rows, before, weights):
    index = lax.broadcasted_iota(jnp.int32, rows.shape, 0)
    back_one = jnp.where(index == 0, before[1:2], pltpu.roll(rows, 1, 0))
    back_two = jnp.where(
        index == 0, before[0:1], jnp.where(index == 1, before[1:2], pltpu.roll(rows, 2, 0))
    )
    return weights[0:1] * rows + weights[1:2] * back_one + weights[2:3] * back_two


def edges_of(first, small, edge):
    return jnp.where(first, small[10:16], edge[0:6])


def product_kernel(first_ref, key_ref, value_ref, edge_ref, small_ref, out_ref):
    first = first_ref[0] != 0
    for g in range(WIDTH // 128):
        cols = pl.ds(g * 128, 128)
        small = small_ref[g].astype(F32)
        edge = edges_of(first, small, edge_ref[:, cols].astype(F32))
        key = featurize(key_ref[:, cols].astype(F32), edge[2:4], small[3:6])
        value = featurize(value_ref[:, cols].astype(F32), edge[4:6], small[6:9])
        out_ref[:, cols] = (key * value).astype(BF)


def filter_kernel(
    first_ref,
    query_ref,
    edge_ref,
    small_ref,
    own_ref,
    halo_ref,
    wide_ref,
    fwd_hi_ref,
    fwd_lo_ref,
    inv_hi_ref,
    inv_lo_ref,
    out_ref,
):
    first = first_ref[0] != 0
    for g in range(WIDTH // 128):
        cols = pl.ds(g * 128, 128)
        small = small_ref[g].astype(F32)
        edge = edges_of(first, small, edge_ref[:, cols].astype(F32))
        query = featurize(query_ref[:, cols].astype(F32), edge[0:2], small[0:3])
        own = own_ref[:, cols]
        prior = wide_ref[g, 128:256].astype(F32)
        before = jnp.where(first, prior, halo_ref[:, cols].astype(F32)).astype(BF)
        signal = jnp.concatenate([before, own], axis=0)
        taps = wide_ref[g, 0:128]
        spec_x = dot(fwd_hi_ref[...], signal) + dot(fwd_lo_ref[...], signal)
        spec_h = dot_nt(fwd_hi_ref[:, 0:128], taps) + dot_nt(fwd_lo_ref[:, 0:128], taps)
        xc, xs, hc, hs = spec_x[:128], spec_x[128:], spec_h[:128], spec_h[128:]
        spec_y = jnp.concatenate([xc * hc - xs * hs, xc * hs + xs * hc], axis=0)
        y_hi = spec_y.astype(BF)
        y_lo = (spec_y - y_hi.astype(F32)).astype(BF)
        inv_hi = inv_hi_ref[...]
        filtered = dot(inv_hi, y_hi) + dot(inv_hi, y_lo) + dot(inv_lo_ref[...], y_hi)
        mixed = query * (filtered + small[9:10] * own.astype(F32))
        out_ref[:, cols] = mixed.astype(BF)


def shift_by_one(value, axes, count):
    return lax.ppermute(value, axes, [(i, (i + 1) % count) for i in range(count)])


def spread(value, axis, count):
    copies = jnp.broadcast_to(value[None], (count,) + value.shape)
    return lax.all_to_all(copies, axis, split_axis=0, concat_axis=0, tiled=True)


def whole(shape):
    return pl.BlockSpec(shape, lambda j: (0,) * len(shape))


def body(
    query_rows, key_rows, value_rows, short_taps, long_taps, skip_gain, prior_qkv, prior_product
):
    n_x, n_z = lax.axis_size("ctx_x"), lax.axis_size("ctx_z")
    n_ctx = n_x * n_z
    n_section = lax.axis_size("section")
    rows, channels = query_rows.shape
    ctx = ("ctx_x", "ctx_z")
    first = (lax.axis_index(ctx) == 0).astype(jnp.int32).reshape(1)

    small = jnp.concatenate(
        [short_taps[0].reshape(9, 128), skip_gain, prior_qkv[0].reshape(6, 128)], axis=0
    )
    smalls = spread(small, ctx, n_ctx)
    last = jnp.concatenate(
        [query_rows[-2:], key_rows[-2:], value_rows[-2:], value_rows[-2:]], axis=0
    )
    edge = shift_by_one(last, ctx, n_ctx)
    wide = jnp.concatenate(
        [long_taps[0], jnp.zeros((1, 128), BF), prior_product[0]], axis=0
    )
    wides = spread(spread(wide, "ctx_z", n_z), "ctx_x", n_x).reshape(n_ctx, 256, 128)

    (fwd_hi, fwd_lo), (inv_hi, inv_lo) = dft_matrices()
    span = channels // CHUNKS
    steps = span // WIDTH
    groups = WIDTH // 128
    smem = pl.BlockSpec(memory_space=pltpu.SMEM)
    params = pltpu.CompilerParams(vmem_limit_bytes=48 * 1024 * 1024)

    def at(chunk):
        return lambda j: (0, chunk * steps + j)

    def at_group(chunk):
        return lambda j: (chunk * steps + j, 0, 0)

    products = []
    for chunk in range(CHUNKS):
        products.append(
            pl.pallas_call(
                product_kernel,
                grid=(steps,),
                in_specs=[
                    smem,
                    pl.BlockSpec((rows, WIDTH), at(chunk)),
                    pl.BlockSpec((rows, WIDTH), at(chunk)),
                    pl.BlockSpec((8, WIDTH), at(chunk)),
                    pl.BlockSpec((groups, 16, 128), at_group(chunk)),
                ],
                out_specs=pl.BlockSpec((rows, WIDTH), lambda j: (0, j)),
                out_shape=jax.ShapeDtypeStruct((rows, span), BF),
                compiler_params=params,
                name="gated_product",
            )(first, key_rows, value_rows, edge, smalls)
        )
    halos = [shift_by_one(product, ctx, n_ctx) for product in products]
    handed = []
    for chunk in range(CHUNKS):
        mixed = pl.pallas_call(
            filter_kernel,
            grid=(steps,),
            in_specs=[
                smem,
                pl.BlockSpec((rows, WIDTH), at(chunk)),
                pl.BlockSpec((8, WIDTH), at(chunk)),
                pl.BlockSpec((groups, 16, 128), at_group(chunk)),
                pl.BlockSpec((rows, WIDTH), lambda j: (0, j)),
                pl.BlockSpec((rows, WIDTH), lambda j: (0, j)),
                pl.BlockSpec((groups, 256, 128), at_group(chunk)),
                whole((256, 256)),
                whole((256, 256)),
                whole((128, 256)),
                whole((128, 256)),
            ],
            out_specs=pl.BlockSpec((rows, WIDTH), lambda j: (0, j)),
            out_shape=jax.ShapeDtypeStruct((rows, span), BF),
            compiler_params=params,
            name="filter_and_gate",
        )(
            first, query_rows, edge, smalls, products[chunk], halos[chunk], wides,
            fwd_hi, fwd_lo, inv_hi, inv_lo,
        )
        handed.append(shift_by_one(mixed, "section", n_section))
    return jnp.concatenate(handed, axis=1)


def solution(mesh):
    n_ctx = mesh.shape["ctx"]
    n_z = 8
    inner = Mesh(
        mesh.devices.reshape(mesh.shape["section"], n_ctx // n_z, n_z), ("section", "ctx_x", "ctx_z")
    )
    ctx = ("ctx_x", "ctx_z")
    in_specs = (
        P(("section",) + ctx, None),
        P(("section",) + ctx, None),
        P(("section",) + ctx, None),
        P("section", None, None, ctx),
        P("section", ctx, None),
        P("section", ctx),
        P("section", None, None, ctx),
        P("section", None, ctx),
    )
    out_specs = P(("section",) + ctx, None)
    return jax.shard_map(body, mesh=inner, in_specs=in_specs, out_specs=out_specs, check_vma=False)
```

time: 186 us -> 128 us (0.69)
  local copies, waits for them, and re-layouts: 60 us -> 12.8 us
  Pallas kernels: 0 us -> 16.7 us
  blocking collectives: 32.4 us -> 18.8 us
  matrix products: 6.9 us -> 0 us
  other arithmetic: 7.12 us -> 2.67 us
  starting transfers between devices: 28.5 us -> 24.1 us
  waiting for transfers between devices: 49.3 us -> 52.3 us
    pallas_call x0 -> x4, Pallas kernels: none -> 16.7 us  [the longest x2 13.7 us: body(): pl.pallas_call(filter_kernel, grid=(steps,), in_specs=[smem, pl.BlockSpec...]
    another operation x2, local copies, waits for them, and re-layouts: 17.4 us -> 1.39 us  [the longest x1 0.7 us: body(): short_taps[0].reshape(9, 128)]
    ppermute x1 -> x5, waiting for transfers between devices: 15.4 us -> 30.5 us  [shift_by_one(): lax.ppermute(value, axes, [(i, (i + 1) % count) for i in range(count)])]
    all_to_all x1, blocking collectives: 32.4 us -> 18.8 us  [spread(): return lax.all_to_all(copies, axis, split_axis=0, concat_axis=0, tiled=True)]
    all_to_all x3 -> x2, waiting for transfers between devices: 33.8 us -> 21.8 us  [spread(): return lax.all_to_all(copies, axis, split_axis=0, concat_axis=0, tiled=True)]
    all_to_all x3 -> x2, starting transfers between devices: 28.5 us -> 16.9 us  [spread(): return lax.all_to_all(copies, axis, split_axis=0, concat_axis=0, tiled=True)]
    slice x2 -> x3, local copies, waits for them, and re-layouts: 13.1 us -> 1.75 us  [the longest x1 0.86 us: body(): query_rows[-2:]]
    unnamed x24 -> x22, local copies, waits for them, and re-layouts: 18 us -> 7.09 us
  transfers between devices with their start and end apart: 4 -> 7, of which waited for: 3 -> 6; matrix products, arithmetic and copies ran while one was open for 30% -> 2% of each run, Pallas kernels for 0% -> 13%
where the time goes in v1:
time: 128 us
  waiting for transfers between devices  52.3 us (41%)
  starting transfers between devices  24.1 us (19%)
  blocking collectives  18.8 us (15%)
  Pallas kernels  16.7 us (13%)
  local copies, waits for them, and re-layouts  12.8 us (10%)
  other arithmetic  2.67 us (2%)
    ppermute x5, waiting for transfers between devices, shift_by_one(): lax.ppermute(value, axes, [(i, (i + 1) % count) for i in range(count)])  30.5 us
    all_to_all x2, waiting for transfers between devices, spread(): return lax.all_to_all(copies, axis, split_axis=0, concat_axis=0, tiled=True)  21.8 us
    all_to_all x1, blocking collectives, spread(): return lax.all_to_all(copies, axis, split_axis=0, concat_axis=0, tiled=True)  18.8 us
    all_to_all x2, starting transfers between devices, spread(): return lax.all_to_all(copies, axis, split_axis=0, concat_axis=0, tiled=True)  16.9 us
    pallas_call x2, Pallas kernels, body(): pl.pallas_call(filter_kernel, grid=(steps,), in_specs=[smem, pl.BlockSpec...  13.7 us
    ppermute x5, starting transfers between devices, shift_by_one(): lax.ppermute(value, axes, [(i, (i + 1) % count) for i in range(count)])  7.21 us
    unnamed x22, local copies, waits for them, and re-layouts  7.09 us
    pallas_call x2, Pallas kernels, body(): pl.pallas_call(product_kernel, grid=(steps,), in_specs=[smem, pl.BlockSpe...  3.02 us
  transfers between devices with their start and end apart: 7, of which 6 were waited for; matrix products, arithmetic and copies ran while one was open for 2% of the time, Pallas kernels for 13%

profile of v1, /device:TPU:32, one launch (start us, length us, event | category | flops | bytes accessed | tf_op | source)
XLA Modules:
  0.0 127.6 jit_solution(17638538227590880782)
XLA Ops:
  0.0 0.7 reshape_squeeze.6
  0.7 0.7 reshape_squeeze.7
  2.1 0.7 broadcast_in_dim.8
  2.7 13.2 %all-to-all-start = ((bf16[32,16,128]{2,1,0:T(8,128)(2,1)}), bf16[32,16,128]{2,1,0:T(8,128)(2,1)S(1)}, u32[]{:S(2)}, u32[]{:S(2)}) async-start(bf16[32,16,128]{2,1,0:T(8,128)(2,1)} %broadcast_in_dim.8), calls=%async_computation | async-start | bytes 262144 | tf_op jit(solution)/shard_map/all_to_all | solution.py:106
  15.9 0.9 pad_maximum_fusion.2
  16.8 9.4 %all-to-all-done.small_ref = bf16[32,16,128]{2,1,0:T(8,128)(2,1)S(1)} async-done(((bf16[32,16,128]{2,1,0:T(8,128)(2,1)}), bf16[32,16,128]{2,1,0:T(8,128)(2,1)S(1)}, u32[]{:S(2)}, u32[]{:S(2)}) %all-to-all-start) | async-done | bytes 131104 | tf_op jit(solution)/shard_map/all_to_all | solution.py:106
  26.3 18.8 %all_to_all.15 = bf16[8,256,128]{2,1,0:T(8,128)(2,1)S(1)} all-to-all(bf16[8,256,128]{2,1,0:T(8,128)(2,1)S(1)} %broadcast_in_dim.10), channel_id=1, replica_groups=mesh['section'=16,'ctx_x'=4,'ctx_z'=8] {'ctx_z'}, dimensions={0} | all-to-all | bytes 1048576 | tf_op jit(solution)/shard_map/all_to_all | solution.py:106
  45.1 1.8 %broadcast_in_dim.11 = bf16[4,8,256,128]{3,2,1,0:T(8,128)(2,1)} broadcast(bf16[8,256,128]{2,1,0:T(8,128)(2,1)S(1)} %all_to_all.15), dimensions={1,2,3} | broadcast | bytes 2621440 | tf_op jit(solution)/shard_map/broadcast_in_dim | solution.py:105
  46.9 3.7 %all-to-all-start.2 = ((bf16[4,8,256,128]{3,2,1,0:T(8,128)(2,1)}), bf16[4,8,256,128]{3,2,1,0:T(8,128)(2,1)S(1)}, u32[]{:S(2)}, u32[]{:S(2)}) async-start(bf16[4,8,256,128]{3,2,1,0:T(8,128)(2,1)} %broadcast_in_dim.11), calls=%async_computation.2 | async-start | bytes 4194304 | tf_op jit(solution)/shard_map/all_to_all | solution.py:106
  50.6 0.9 slice.10
  51.5 0.9 slice.11
  52.5 2.5 %collective-permute-start = (bf16[8,4096]{1,0:T(8,128)(2,1)S(1)}, bf16[8,4096]{1,0:T(8,128)(2,1)S(1)}, u32[]{:S(2)}, u32[]{:S(2)}) collective-permute-start(bf16[8,4096]{1,0:T(8,128)(2,1)S(1)} %pad_maximum_fusion.1), channel_id=1, source_target_pairs={{0,1},{1,2},{2,3},{3,4},{4,5},{5,6},{6,7},{7,8},{8,9},{9,10},{10,1... | collective-permute-start | bytes 196616 | tf_op jit(solution)/shard_map/ppermute | solution.py:101
  55.0 7.4 %collective-permute-done.edge_ref = bf16[8,4096]{1,0:T(8,128)(2,1)S(1)} collective-permute-done((bf16[8,4096]{1,0:T(8,128)(2,1)S(1)}, bf16[8,4096]{1,0:T(8,128)(2,1)S(1)}, u32[]{:S(2)}, u32[]{:S(2)}) %collective-permute-start) | collective-permute-done | bytes 65568 | tf_op jit(solution)/shard_map/ppermute | solution.py:101
  62.4 1.2 copy-done.1
  63.7 1.0 gated_product.2.own_ref
  64.7 2.1 %collective-permute-start.1 = (bf16[128,2048]{1,0:T(8,128)(2,1)S(1)}, bf16[128,2048]{1,0:T(8,128)(2,1)S(1)}, u32[]{:S(2)}, u32[]{:S(2)}) collective-permute-start(bf16[128,2048]{1,0:T(8,128)(2,1)S(1)} %gated_product.2.own_ref), channel_id=1, source_target_pairs={{0,1},{1,2},{2,3},{3,4},{4,5},{5,6},{6,7},{7,8},{8,9},{9,10},{10,1... | collective-permute-start | bytes 1572872 | tf_op jit(solution)/shard_map/ppermute | solution.py:101
  66.7 2.0 %gated_product.3.own_ref = bf16[128,2048]{1,0:T(8,128)(2,1)} custom-call(s32[1]{0:T(128)} %bitcast.first_ref, bf16[128,4096]{1,0:T(8,128)(2,1)S(1)} %copy-done.1, bf16[128,4096]{1,0:T(8,128)(2,1)S(1)} %copy-done, bf16[8,4096]{1,0:T(8,128)(2,1)S(1)} %collective-permute-done.edge_ref, bf16[32,16,128]{2,1,0:T(8,128)(2,1)S(1)} %all-to-all-done.small_ref), custom_call_target="tpu_custom_call" | custom-call | tf_op jit(solution)/shard_map/gated_product/pallas_call | solution.py:152
  68.8 1.9 %collective-permute-start.3 = (bf16[128,2048]{1,0:T(8,128)(2,1)}, bf16[128,2048]{1,0:T(8,128)(2,1)S(1)}, u32[]{:S(2)}, u32[]{:S(2)}) collective-permute-start(bf16[128,2048]{1,0:T(8,128)(2,1)} %gated_product.3.own_ref), channel_id=1, source_target_pairs={{0,1},{1,2},{2,3},{3,4},{4,5},{5,6},{6,7},{7,8},{8,9},{9,10},{10,1... | collective-permute-start | bytes 1572872 | tf_op jit(solution)/shard_map/ppermute | solution.py:101
  70.7 14.0 %collective-permute-done.1.halo_ref = bf16[128,2048]{1,0:T(8,128)(2,1)S(1)} collective-permute-done((bf16[128,2048]{1,0:T(8,128)(2,1)S(1)}, bf16[128,2048]{1,0:T(8,128)(2,1)S(1)}, u32[]{:S(2)}, u32[]{:S(2)}) %collective-permute-start.1) | collective-permute-done | bytes 524320 | tf_op jit(solution)/shard_map/ppermute | solution.py:101
  84.7 0.8 copy-done.7
  85.5 12.4 %all-to-all-done.2 = bf16[4,8,256,128]{3,2,1,0:T(8,128)(2,1)S(1)} async-done(((bf16[4,8,256,128]{3,2,1,0:T(8,128)(2,1)}), bf16[4,8,256,128]{3,2,1,0:T(8,128)(2,1)S(1)}, u32[]{:S(2)}, u32[]{:S(2)}) %all-to-all-start.2) | async-done | bytes 2097184 | tf_op jit(solution)/shard_map/all_to_all | solution.py:106
  97.9 1.2 copy-done.2
  99.1 1.0 copy-done.4
  100.2 0.9 copy-done.6
  101.1 1.0 copy-done.8
  102.1 0.8 copy-done.10
  103.0 6.4 %filter_and_gate.2 = bf16[128,2048]{1,0:T(8,128)(2,1)S(1)} custom-call(s32[1]{0:T(128)} %bitcast.first_ref, bf16[128,4096]{1,0:T(8,128)(2,1)S(1)} %copy-done.2, bf16[8,4096]{1,0:T(8,128)(2,1)S(1)} %collective-permute-done.edge_ref, bf16[32,16,128]{2,1,0:T(8,128)(2,1)S(1)} %all-to-all-done.small_ref, bf16[128,2048]{1,0:T(8,128)(2,1)S(1)} %copy-done.4, ...), custom_call_target="tpu_custom_call" | custom-call | tf_op jit(solution)/shard_map/filter_and_gate/pallas_call | solution.py:171
  109.4 7.3 %filter_and_gate.3 = bf16[128,2048]{1,0:T(8,128)(2,1)S(1)} custom-call(s32[1]{0:T(128)} %bitcast.first_ref, bf16[128,4096]{1,0:T(8,128)(2,1)S(1)} %copy-done.2, bf16[8,4096]{1,0:T(8,128)(2,1)S(1)} %collective-permute-done.edge_ref, bf16[32,16,128]{2,1,0:T(8,128)(2,1)S(1)} %all-to-all-done.small_ref, bf16[128,2048]{1,0:T(8,128)(2,1)} %gated_product.3.own_ref, ...), custom_call_target="tpu_custom_call" | custom-call | tf_op jit(solution)/shard_map/filter_and_gate/pallas_call | solution.py:171
  116.7 0.8 collective-permute-start.4
  117.5 1.7 %collective-permute-done.2 = bf16[128,2048]{1,0:T(8,128)(2,1)S(1)} collective-permute-done((bf16[128,2048]{1,0:T(8,128)(2,1)S(1)}, bf16[128,2048]{1,0:T(8,128)(2,1)S(1)}, u32[]{:S(2)}, u32[]{:S(2)}) %collective-permute-start.2) | collective-permute-done | bytes 524320 | tf_op jit(solution)/shard_map/ppermute | solution.py:101
  119.2 7.3 %collective-permute-done.4 = bf16[128,2048]{1,0:T(8,128)(2,1)S(1)} collective-permute-done((bf16[128,2048]{1,0:T(8,128)(2,1)S(1)}, bf16[128,2048]{1,0:T(8,128)(2,1)S(1)}, u32[]{:S(2)}, u32[]{:S(2)}) %collective-permute-start.4) | collective-permute-done | bytes 524320 | tf_op jit(solution)/shard_map/ppermute | solution.py:101
  126.5 1.1 pad_maximum_fusion
  (22 shorter events, 0.9 us)
Async XLA Ops:
  2.7 23.4 %all-to-all-start = ((bf16[32,16,128]{2,1,0:T(8,128)(2,1)}), bf16[32,16,128]{2,1,0:T(8,128)(2,1)S(1)}, u32[]{:S(2)}, u32[]{:S(2)}) async-start(bf16[32,16,128]{2,1,0:T(8,128)(2,1)} %broadcast_in_dim.8), calls=%async_computation | async-start | bytes 262144 | tf_op jit(solution)/shard_map/all_to_all | solution.py:106
  46.9 5.5 %copy-start = (bf16[128,4096]{1,0:T(8,128)(2,1)S(1)}, bf16[128,4096]{1,0:T(8,128)(2,1)}, u32[]{:S(2)}) copy-start(bf16[128,4096]{1,0:T(8,128)(2,1)} %value_ref.3) | copy-start | bytes 3145732
  46.9 51.0 %all-to-all-start.2 = ((bf16[4,8,256,128]{3,2,1,0:T(8,128)(2,1)}), bf16[4,8,256,128]{3,2,1,0:T(8,128)(2,1)S(1)}, u32[]{:S(2)}, u32[]{:S(2)}) async-start(bf16[4,8,256,128]{3,2,1,0:T(8,128)(2,1)} %broadcast_in_dim.11), calls=%async_computation.2 | async-start | bytes 4194304 | tf_op jit(solution)/shard_map/all_to_all | solution.py:106
  52.5 9.9 %collective-permute-start = (bf16[8,4096]{1,0:T(8,128)(2,1)S(1)}, bf16[8,4096]{1,0:T(8,128)(2,1)S(1)}, u32[]{:S(2)}, u32[]{:S(2)}) collective-permute-start(bf16[8,4096]{1,0:T(8,128)(2,1)S(1)} %pad_maximum_fusion.1), channel_id=1, source_target_pairs={{0,1},{1,2},{2,3},{3,4},{4,5},{5,6},{6,7},{7,8},{8,9},{9,10},{10,1... | collective-permute-start | bytes 196616 | tf_op jit(solution)/shard_map/ppermute | solution.py:101
  62.4 1.2 copy-start.1
  64.6 6.0 %copy-start.3 = (bf16[128,2048]{1,0:T(8,128)(2,1)}, bf16[128,2048]{1,0:T(8,128)(2,1)S(1)}, u32[]{:S(2)}) copy-start(bf16[128,2048]{1,0:T(8,128)(2,1)S(1)} %gated_product.2.own_ref) | copy-start | bytes 1572868
  64.7 33.3 %copy-start.5 = (bf16[256,256]{1,0:T(8,128)(2,1)S(1)}, bf16[256,256]{1,0:T(8,128)(2,1)}, u32[]{:S(2)}) copy-start(bf16[256,256]{1,0:T(8,128)(2,1)} %constant.22.clone.fwd_hi_ref) | copy-start | bytes 393220
  64.7 33.3 %copy-start.9 = (bf16[128,256]{1,0:T(8,128)(2,1)S(1)}, bf16[128,256]{1,0:T(8,128)(2,1)}, u32[]{:S(2)}) copy-start(bf16[128,256]{1,0:T(8,128)(2,1)} %constant.24.clone.inv_hi_ref) | copy-start | bytes 196612
  64.7 20.0 %collective-permute-start.1 = (bf16[128,2048]{1,0:T(8,128)(2,1)S(1)}, bf16[128,2048]{1,0:T(8,128)(2,1)S(1)}, u32[]{:S(2)}, u32[]{:S(2)}) collective-permute-start(bf16[128,2048]{1,0:T(8,128)(2,1)S(1)} %gated_product.2.own_ref), channel_id=1, source_target_pairs={{0,1},{1,2},{2,3},{3,4},{4,5},{5,6},{6,7},{7,8},{8,9},{9,10},{10,1... | collective-permute-start | bytes 1572872 | tf_op jit(solution)/shard_map/ppermute | solution.py:101
  68.8 40.6 %collective-permute-start.3 = (bf16[128,2048]{1,0:T(8,128)(2,1)}, bf16[128,2048]{1,0:T(8,128)(2,1)S(1)}, u32[]{:S(2)}, u32[]{:S(2)}) collective-permute-start(bf16[128,2048]{1,0:T(8,128)(2,1)} %gated_product.3.own_ref), channel_id=1, source_target_pairs={{0,1},{1,2},{2,3},{3,4},{4,5},{5,6},{6,7},{7,8},{8,9},{9,10},{10,1... | collective-permute-start | bytes 1572872 | tf_op jit(solution)/shard_map/ppermute | solution.py:101
  84.7 0.8 copy-start.7
  97.9 1.2 copy-start.2
  99.1 1.0 copy-start.4
  100.2 0.9 copy-start.6
  101.1 1.0 copy-start.8
  102.1 0.8 copy-start.10
  109.4 9.8 %collective-permute-start.2 = (bf16[128,2048]{1,0:T(8,128)(2,1)S(1)}, bf16[128,2048]{1,0:T(8,128)(2,1)S(1)}, u32[]{:S(2)}, u32[]{:S(2)}) collective-permute-start(bf16[128,2048]{1,0:T(8,128)(2,1)S(1)} %filter_and_gate.2), channel_id=1, source_target_pairs={{0,32},{32,64},{64,96},{96,128},{128,160},{160,192},{192,224},{224... | collective-permute-start | bytes 1572872 | tf_op jit(solution)/shard_map/ppermute | solution.py:101
  116.7 9.8 %collective-permute-start.4 = (bf16[128,2048]{1,0:T(8,128)(2,1)S(1)}, bf16[128,2048]{1,0:T(8,128)(2,1)S(1)}, u32[]{:S(2)}, u32[]{:S(2)}) collective-permute-start(bf16[128,2048]{1,0:T(8,128)(2,1)S(1)} %filter_and_gate.3), channel_id=1, source_target_pairs={{0,32},{32,64},{64,96},{96,128},{128,160},{160,192},{192,224},{224... | collective-permute-start | bytes 1572872 | tf_op jit(solution)/shard_map/ppermute | solution.py:101

commit v2 on v1

v2 whole, which is shorter than its diff:
```python
import functools

import jax
import jax.numpy as jnp
import numpy as np
from jax import lax
from jax.experimental import pallas as pl
from jax.experimental.pallas import tpu as pltpu
from jax.sharding import Mesh
from jax.sharding import PartitionSpec as P

BF = jnp.bfloat16
F32 = jnp.float32
STEP = 512
BLOCKS = ((0, 1), (2, 3))
HINT = 20 * 10**9


def stacked_hi_lo(matrix):
    high = matrix.astype(np.float32).astype(BF)
    low = (matrix - high.astype(np.float64)).astype(np.float32).astype(BF)
    return np.concatenate([high, low], axis=0)


def dft_matrices():
    n = np.arange(256, dtype=np.float64)[None, :]
    k = np.arange(128, dtype=np.float64)[:, None]
    angle = np.pi * (2 * k + 1) * n / 256
    forward = np.concatenate([np.cos(angle), np.sin(angle)], axis=0)
    inverse = forward.T[128:] / 128
    return stacked_hi_lo(forward), stacked_hi_lo(inverse)


def dot(a, b):
    return lax.dot_general(a, b, (((1,), (0,)), ((), ())), preferred_element_type=F32)


def dot_nt(a, b):
    return lax.dot_general(a, b, (((1,), (1,)), ((), ())), preferred_element_type=F32)


def featurize(rows, before, weights):
    index = lax.broadcasted_iota(jnp.int32, rows.shape, 0)
    back_one = jnp.where(index == 0, before[1:2], pltpu.roll(rows, 1, 0))
    back_two = jnp.where(
        index == 0, before[0:1], jnp.where(index == 1, before[1:2], pltpu.roll(rows, 2, 0))
    )
    return weights[0:1] * rows + weights[1:2] * back_one + weights[2:3] * back_two


def edges_of(first, small, edge):
    return jnp.where(first, small[10:16], edge[0:6])


def small_at(ref, start, count):
    parts = []
    for g in range(start, start + count):
        low = 128 + 16 * (g // 8)
        parts.append(ref[g % 8, low : low + 16].astype(F32))
    return jnp.concatenate(parts, axis=1)


def lanes(ref, start, count):
    return jnp.concatenate([ref[start + i].astype(F32) for i in range(count)], axis=1)


def prepare_kernel(
    query_ref, key_ref, value_ref, short_ref, gain_ref, qkv_ref, prior_ref,
    edge_ref, small_ref, tail_ref,
):
    ends = [ref[...].astype(F32)[6:8] for ref in (query_ref, key_ref, value_ref)]
    edge_ref[...] = jnp.concatenate(ends + ends[2:], axis=0).astype(BF)
    parts = [short_ref[0, m].astype(F32) for m in range(3)] + [gain_ref[...].astype(F32)]
    parts += [qkv_ref[0, m].astype(F32) for m in range(3)]
    small = jnp.concatenate(parts, axis=0).astype(BF)
    prior = jnp.concatenate([jnp.zeros((1, 128), F32), prior_ref[0].astype(F32)], axis=0)
    tail_ref[0] = prior.astype(BF)
    for i in range(small_ref.shape[0]):
        small_ref[i] = small


def spread_kernel(small_ref, taps_ref, out_ref):
    for i in range(out_ref.shape[0]):
        out_ref[i, 0:128] = taps_ref[0]
        for x in range(4):
            out_ref[i, 128 + 16 * x : 144 + 16 * x] = small_ref[x]


def product_of(key, value, edge, small):
    key = featurize(key.astype(F32), edge[0:2], small[3:6])
    value = featurize(value.astype(F32), edge[2:4], small[6:9])
    return (key * value).astype(BF)


def product_kernel(blocks, flags_ref, key_ref, value_ref, edge_ref, small_ref, out_ref):
    first = flags_ref[0] == 0
    groups = STEP // 128
    for s in range(out_ref.shape[1] // STEP):
        cols = pl.ds(blocks[0] * 1024 + s * STEP, STEP)
        small = small_at(small_ref, blocks[0] * 8 + s * groups, groups)
        edge = edges_of(first, small, edge_ref[:, cols].astype(F32))
        product = product_of(key_ref[:, cols], value_ref[:, cols], edge[2:6], small)
        out_ref[:, pl.ds(s * STEP, STEP)] = product


def choose_taps(flags_ref, blocks, taps_refs, taps_ref):
    index, x = flags_ref[0], flags_ref[1]
    edge = jnp.where(index & 7 == 0, 1, 0)
    for place, block in enumerate(blocks):
        which = (block - x) & 3
        which = jnp.where(which == 3, 3 + edge, which)
        for step, ref in enumerate(taps_refs):

            @pl.when(which == step)
            def _():
                taps_ref[place * 8 : place * 8 + 8] = ref[:, 0:128]


def spectrum_of(before, own, forward_ref):
    signal = jnp.concatenate([before, own], axis=0)
    spectrum = dot(forward_ref[...], signal)
    return spectrum[:256] + spectrum[256:]


def spectrum_kernel(own_ref, halo_ref, forward_ref, out_ref):
    for s in range(out_ref.shape[1] // STEP):
        here = pl.ds(s * STEP, STEP)
        out_ref[:, here] = spectrum_of(halo_ref[:, here], own_ref[:, here], forward_ref)


def filter_kernel(blocks, flags_ref, query_ref, edge_ref, small_ref, own_ref, spec_ref, *refs):
    prior_refs, refs = refs[: len(blocks)], refs[len(blocks) :]
    taps_refs, (forward_ref, inverse_ref, out_ref, taps_ref, both_ref) = refs[:5], refs[5:]
    first = flags_ref[0] == 0

    @pl.when(first)
    def _():
        for s in range(out_ref.shape[1] // STEP):
            here = pl.ds(s * STEP, STEP)
            prior = []
            for i in range(STEP // 128):
                place, z = divmod(s * STEP // 128 + i, 8)
                prior.append(prior_refs[place][z])
            prior = jnp.concatenate(prior, axis=1)
            both_ref[:, here] = spectrum_of(prior, own_ref[:, here], forward_ref)

    @pl.when(jnp.logical_not(first))
    def _():
        both_ref[...] = spec_ref[...]

    choose_taps(flags_ref, blocks, taps_refs, taps_ref)
    groups = STEP // 128
    for s in range(out_ref.shape[1] // STEP):
        here = pl.ds(s * STEP, STEP)
        cols = pl.ds(blocks[0] * 1024 + s * STEP, STEP)
        small = small_at(small_ref, blocks[0] * 8 + s * groups, groups)
        edge = edges_of(first, small, edge_ref[:, cols].astype(F32))
        query = featurize(query_ref[:, cols].astype(F32), edge[0:2], small[0:3])
        taps = taps_ref[pl.ds(s * groups, groups)].reshape(STEP, 128)
        spec_h = dot_nt(forward_ref[:, 0:128], taps)
        spec_h = spec_h[:256] + spec_h[256:]
        xc, xs = both_ref[0:128, here], both_ref[128:256, here]
        hc, hs = spec_h[:128], spec_h[128:]
        spec_y = jnp.concatenate([xc * hc - xs * hs, xc * hs + xs * hc], axis=0)
        y_hi = spec_y.astype(BF)
        y_lo = (spec_y - y_hi.astype(F32)).astype(BF)
        both = dot(inverse_ref[...], y_hi)
        filtered = both[:128] + both[128:] + dot(inverse_ref[0:128, :], y_lo)
        own = own_ref[:, here].astype(F32)
        out_ref[:, here] = (query * (filtered + small[9:10] * own)).astype(BF)


def shift_by_one(value, axes, count):
    return lax.ppermute(value, axes, [(i, (i + 1) % count) for i in range(count)])


def exchange(copies, axis):
    return lax.all_to_all(copies, axis, split_axis=0, concat_axis=0, tiled=True)


def whole(shape):
    return pl.BlockSpec(shape, lambda *_: (0,) * len(shape))


def body(
    query_rows, key_rows, value_rows, short_taps, long_taps, skip_gain, prior_qkv, prior_product
):
    n_x, n_z = lax.axis_size("ctx_x"), lax.axis_size("ctx_z")
    n_ctx = n_x * n_z
    n_section = lax.axis_size("section")
    rows, channels = query_rows.shape
    ctx = ("ctx_x", "ctx_z")
    flags = jnp.stack([lax.axis_index(ctx), lax.axis_index("ctx_x")]).astype(jnp.int32)
    params = pltpu.CompilerParams(vmem_limit_bytes=24 * 1024 * 1024)
    smem = pl.BlockSpec(memory_space=pltpu.SMEM)
    vmem = pl.BlockSpec(memory_space=pltpu.VMEM)

    def in_hbm(value):
        return pltpu.with_memory_space_constraint(value, pltpu.HBM)

    last_rows = pl.BlockSpec((8, channels), lambda j: (rows // 8 - 1, 0))
    prepared = [(8, channels), (n_x, 16, 128), (1, 128, 128)]
    edge_own, small_own, tail = pl.pallas_call(
        prepare_kernel,
        grid=(1,),
        in_specs=[
            last_rows,
            last_rows,
            last_rows,
            whole(short_taps.shape),
            whole(skip_gain.shape),
            whole(prior_qkv.shape),
            whole(prior_product.shape),
        ],
        out_specs=[whole(shape) for shape in prepared],
        out_shape=[jax.ShapeDtypeStruct(shape, BF) for shape in prepared],
        compiler_params=params,
        name="prepare",
    )(
        *map(in_hbm, (query_rows, key_rows, value_rows)),
        *map(in_hbm, (short_taps, skip_gain, prior_qkv, prior_product)),
    )

    def send(value, pairs):
        return lax.ppermute(value, ctx, pairs)

    def shift(value, steps):
        return send(value, [(i, (i + steps) % n_ctx) for i in range(n_ctx)])

    def shift_x(value, steps):
        return lax.ppermute(value, "ctx_x", [(i, (i + steps) % n_x) for i in range(n_x)])

    def send_z(value, step, stops):
        return send(value, [(x * n_z + z + step, x * n_z + z) for x in range(n_x) for z in stops])

    edge = shift(edge_own, 1)
    along_x = exchange(small_own, "ctx_x")
    tails = [tail] + [send_z(tail, step, (0, 4)) for step in (1, 2, 3)]
    tail = jnp.concatenate(tails, axis=0)
    along_x, tail = lax.optimization_barrier((along_x, tail))
    spread = pl.pallas_call(
        spread_kernel,
        in_specs=[vmem, vmem],
        out_specs=vmem,
        out_shape=jax.ShapeDtypeStruct((n_z, 192, 128), BF),
        compiler_params=params,
        name="spread",
    )(along_x, long_taps)
    along_z = exchange(spread, "ctx_z")
    last_tail = send_z(tail, 4, (0,))
    along_z, edge, tail, last_tail = lax.optimization_barrier((along_z, edge, tail, last_tail))
    tail = jnp.concatenate([tail, last_tail], axis=0)

    products, halos = [], []
    for blocks in BLOCKS:
        product = pl.pallas_call(
            functools.partial(product_kernel, blocks),
            in_specs=[smem] + [vmem] * 4,
            out_specs=vmem,
            out_shape=jax.ShapeDtypeStruct((rows, 1024 * len(blocks)), BF),
            compiler_params=params,
            name="gated_product",
        )(flags, key_rows, value_rows, edge, along_z)
        products.append(product)
        halos.append(shift(product, 1))

    taps, tail, *products = lax.optimization_barrier((along_z, tail, *products))
    taps = taps[:, 0:128]
    inner = [(x * n_z + z, (x + 1) % n_x * n_z + z) for x in range(n_x) for z in range(1, n_z)]
    taps_before = send(taps, inner)
    taps_after = send(taps, [(i, (i - n_z) % n_ctx) for i in range(n_ctx)])
    prior_one = send(tail, [(n_z, 0), (2 * n_z, n_z)])
    prior_three = send(tail, [(3 * n_z, 0)])
    taps_after, taps_before, prior_one = lax.optimization_barrier(
        (taps_after, taps_before, prior_one)
    )
    taps_two = send(taps_after, [(i, (i - n_z) % n_ctx) for i in range(n_ctx)])
    taps_first = send(taps_before, [(x * n_z + 1, x * n_z) for x in range(n_x)])
    prior_two = send(prior_one, [(n_z, 0)])
    all_taps = [taps, taps_after, taps_two, taps_before, taps_first]
    priors = [tail, prior_one, prior_two, prior_three]

    forward, inverse = dft_matrices()
    handed = []
    for number, blocks in enumerate(BLOCKS):
        width = 1024 * len(blocks)
        spectrum = pl.pallas_call(
            spectrum_kernel,
            in_specs=[vmem] * 3,
            out_specs=vmem,
            out_shape=jax.ShapeDtypeStruct((256, width), F32),
            compiler_params=params,
            cost_estimate=pl.CostEstimate(
                flops=HINT, bytes_accessed=2 * 256 * width, transcendentals=0
            ),
            name="product_spectrum",
        )(products[number], halos[number], forward)
        mixed = pl.pallas_call(
            functools.partial(filter_kernel, blocks),
            in_specs=[smem] + [vmem] * (12 + len(blocks)),
            out_specs=vmem,
            out_shape=jax.ShapeDtypeStruct((rows, width), BF),
            scratch_shapes=[
                pltpu.VMEM((8 * len(blocks), 128, 128), BF),
                pltpu.VMEM((256, width), F32),
            ],
            compiler_params=params,
            name="filter_and_gate",
        )(
            flags, query_rows, edge, along_z, products[number], spectrum,
            *[priors[x] for x in blocks], *all_taps, forward, inverse,
        )
        handed.append(shift_by_one(mixed, "section", n_section))
    return jnp.concatenate(handed, axis=1)


def solution(mesh):
    n_ctx = mesh.shape["ctx"]
    n_z = 8
    inner = Mesh(
        mesh.devices.reshape(mesh.shape["section"], n_ctx // n_z, n_z), ("section", "ctx_x", "ctx_z")
    )
    ctx = ("ctx_x", "ctx_z")
    in_specs = (
        P(("section",) + ctx, None),
        P(("section",) + ctx, None),
        P(("section",) + ctx, None),
        P("section", None, None, ctx),
        P("section", ctx, None),
        P("section", ctx),
        P("section", None, None, ctx),
        P("section", None, ctx),
    )
    out_specs = P(("section",) + ctx, None)
    return jax.shard_map(body, mesh=inner, in_specs=in_specs, out_specs=out_specs, check_vma=False)
```

time: 128 us -> 95 us (0.74)
  blocking collectives: 18.8 us -> 0 us
  starting transfers between devices: 24.1 us -> 41.3 us
  waiting for transfers between devices: 52.3 us -> 38.3 us
  local copies, waits for them, and re-layouts: 12.8 us -> 0.05 us
  Pallas kernels: 16.7 us -> 13.3 us
  other arithmetic: 2.67 us -> 1.19 us
    ppermute x0 -> x14, starting transfers between devices: none -> 25.5 us  [send(): return lax.ppermute(value, ctx, pairs)]
    ppermute x0 -> x14, waiting for transfers between devices: none -> 24.4 us  [send(): return lax.ppermute(value, ctx, pairs)]
    ppermute x5 -> x2, waiting for transfers between devices: 30.5 us -> 10.9 us  [shift_by_one(): lax.ppermute(value, axes, [(i, (i + 1) % count) for i in range(count)])]
    all_to_all x1 -> x0, blocking collectives: 18.8 us -> none  [spread(): return lax.all_to_all(copies, axis, split_axis=0, concat_axis=0, tiled=True)]
    all_to_all x2, waiting for transfers between devices: 21.8 us -> 3.05 us  [exchange(): return lax.all_to_all(copies, axis, split_axis=0, concat_axis=0, tiled=True)]
    ppermute x5 -> x2, starting transfers between devices: 7.21 us -> 0.04 us  [shift_by_one(): lax.ppermute(value, axes, [(i, (i + 1) % count) for i in range(count)])]
    unnamed x22 -> x12, local copies, waits for them, and re-layouts: 7.09 us -> 0.03 us
    pallas_call x4 -> x8, Pallas kernels: 16.7 us -> 13.3 us  [the longest x2 6.49 us: body(): pl.pallas_call(functools.partial(filter_kernel, blocks), in_specs=[smem]...]
  transfers between devices with their start and end apart: 7 -> 18, of which waited for: 6 -> 11; matrix products, arithmetic and copies ran while one was open for 2% -> 0% of each run, Pallas kernels for 13% -> 10%
where the time goes in v2:
time: 95 us; the launch traced here: 94.4 us
  starting transfers between devices  41.3 us (43%)
  waiting for transfers between devices  38.3 us (40%)
  Pallas kernels  13.3 us (14%)
  other arithmetic  1.19 us (1%)
    ppermute x14, starting transfers between devices, send(): return lax.ppermute(value, ctx, pairs)  25.5 us
    ppermute x14, waiting for transfers between devices, send(): return lax.ppermute(value, ctx, pairs)  24.4 us
    all_to_all x2, starting transfers between devices, exchange(): return lax.all_to_all(copies, axis, split_axis=0, concat_axis=0, tiled=True)  15.8 us
    ppermute x2, waiting for transfers between devices, shift_by_one(): lax.ppermute(value, axes, [(i, (i + 1) % count) for i in range(count)])  10.9 us
    pallas_call x2, Pallas kernels, body(): pl.pallas_call(functools.partial(filter_kernel, blocks), in_specs=[smem]...  6.49 us
    all_to_all x2, waiting for transfers between devices, exchange(): return lax.all_to_all(copies, axis, split_axis=0, concat_axis=0, tiled=True)  3.05 us
    pallas_call x2, Pallas kernels, body(): pl.pallas_call(functools.partial(product_kernel, blocks), in_specs=[smem]...  2.87 us
  transfers between devices with their start and end apart: 18, of which 11 were waited for; matrix products, arithmetic and copies ran while one was open for 0% of the time, Pallas kernels for 10%

profile of v2, /device:TPU:32, one launch (start us, length us, event | category | flops | bytes accessed | tf_op | source)
XLA Modules:
  0.0 94.4 jit_solution(13231826785702710855)
XLA Ops:
  0.0 1.7 %prepare.1 = (bf16[8,4096]{1,0:T(8,128)(2,1)S(1)}, bf16[4,16,128]{2,1,0:T(8,128)(2,1)}, bf16[1,128,128]{2,1,0:T(8,128)(2,1)S(1)}) custom-call(bf16[128,4096]{1,0:T(8,128)(2,1)} %query_ref.5, bf16[128,4096]{1,0:T(8,128)(2,1)} %key_ref.5, bf16[128,4096]{1,0:T(8,128)(2,1)} %value_ref.5, bf16[1,3,3,128]{3,2,1,0:T(4,128)(2,1)} %short_ref.1, ...), custom_call_target="tpu_custom_call" | custom-call | tf_op jit(solution)/shard_map/prepare/pallas_call | solution.py:203
  1.7 1.3 %collective-permute-start = (bf16[1,128,128]{2,1,0:T(8,128)(2,1)S(1)}, bf16[1,128,128]{2,1,0:T(8,128)(2,1)S(1)}, u32[]{:S(2)}, u32[]{:S(2)}) collective-permute-start(bf16[1,128,128]{2,1,0:T(8,128)(2,1)S(1)} %get-tuple-element.22), channel_id=1, source_target_pairs={{1,0},{5,4},{9,8},{13,12},{17,16},{21,20},{25,24},{29,28},{33,32},... | collective-permute-start | bytes 98312 | tf_op jit(solution)/shard_map/ppermute | solution.py:225
  3.0 1.3 %collective-permute-start.1 = (bf16[1,128,128]{2,1,0:T(8,128)(2,1)S(1)}, bf16[1,128,128]{2,1,0:T(8,128)(2,1)S(1)}, u32[]{:S(2)}, u32[]{:S(2)}) collective-permute-start(bf16[1,128,128]{2,1,0:T(8,128)(2,1)S(1)} %get-tuple-element.22), channel_id=1, source_target_pairs={{2,0},{6,4},{10,8},{14,12},{18,16},{22,20},{26,24},{30,28},{34,32}... | collective-permute-start | bytes 98312 | tf_op jit(solution)/shard_map/ppermute | solution.py:225
  4.3 1.3 %collective-permute-start.2 = (bf16[1,128,128]{2,1,0:T(8,128)(2,1)S(1)}, bf16[1,128,128]{2,1,0:T(8,128)(2,1)S(1)}, u32[]{:S(2)}, u32[]{:S(2)}) collective-permute-start(bf16[1,128,128]{2,1,0:T(8,128)(2,1)S(1)} %get-tuple-element.22), channel_id=1, source_target_pairs={{3,0},{7,4},{11,8},{15,12},{19,16},{23,20},{27,24},{31,28},{35,32}... | collective-permute-start | bytes 98312 | tf_op jit(solution)/shard_map/ppermute | solution.py:225
  5.6 4.3 %all-to-all-start = ((bf16[4,16,128]{2,1,0:T(8,128)(2,1)}), bf16[4,16,128]{2,1,0:T(8,128)(2,1)S(1)}, u32[]{:S(2)}, u32[]{:S(2)}) async-start(bf16[4,16,128]{2,1,0:T(8,128)(2,1)} %get-tuple-element.21), calls=%async_computation | async-start | bytes 32768 | tf_op jit(solution)/shard_map/all_to_all | solution.py:178
  9.9 2.3 %collective-permute-done.2 = bf16[1,128,128]{2,1,0:T(8,128)(2,1)S(1)} collective-permute-done((bf16[1,128,128]{2,1,0:T(8,128)(2,1)S(1)}, bf16[1,128,128]{2,1,0:T(8,128)(2,1)S(1)}, u32[]{:S(2)}, u32[]{:S(2)}) %collective-permute-start.2) | collective-permute-done | bytes 32800 | tf_op jit(solution)/shard_map/ppermute | solution.py:225
  12.2 3.0 %all-to-all-done.small_ref = bf16[4,16,128]{2,1,0:T(8,128)(2,1)S(1)} async-done(((bf16[4,16,128]{2,1,0:T(8,128)(2,1)}), bf16[4,16,128]{2,1,0:T(8,128)(2,1)S(1)}, u32[]{:S(2)}, u32[]{:S(2)}) %all-to-all-start) | async-done | bytes 16416 | tf_op jit(solution)/shard_map/all_to_all | solution.py:178
  15.3 0.8 spread.1
  16.1 11.5 %all-to-all-start.1 = ((bf16[8,192,128]{2,1,0:T(8,128)(2,1)}), bf16[8,192,128]{2,1,0:T(8,128)(2,1)S(1)}, u32[]{:S(2)}, u32[]{:S(2)}) async-start(bf16[8,192,128]{2,1,0:T(8,128)(2,1)} %spread.1), calls=%async_computation.1 | async-start | bytes 786432 | tf_op jit(solution)/shard_map/all_to_all | solution.py:178
  27.5 1.3 %collective-permute-start.4 = (bf16[4,128,128]{2,1,0:T(8,128)(2,1)S(1)}, bf16[4,128,128]{2,1,0:T(8,128)(2,1)S(1)}, u32[]{:S(2)}, u32[]{:S(2)}) collective-permute-start(bf16[4,128,128]{2,1,0:T(8,128)(2,1)S(1)} %pad_maximum_fusion.2), channel_id=1, source_target_pairs={{4,0},{12,8},{20,16},{28,24},{36,32},{44,40},{52,48},{60,56},{68,6... | collective-permute-start | bytes 393224 | tf_op jit(solution)/shard_map/ppermute | solution.py:225
  28.8 3.3 %collective-permute-start.3 = (bf16[8,4096]{1,0:T(8,128)(2,1)S(1)}, bf16[8,4096]{1,0:T(8,128)(2,1)S(1)}, u32[]{:S(2)}, u32[]{:S(2)}) collective-permute-start(bf16[8,4096]{1,0:T(8,128)(2,1)S(1)} %get-tuple-element.24), channel_id=1, source_target_pairs={{0,1},{1,2},{2,3},{3,4},{4,5},{5,6},{6,7},{7,8},{8,9},{9,10},{10,1... | collective-permute-start | bytes 196616 | tf_op jit(solution)/shard_map/ppermute | solution.py:225
  32.2 6.9 %collective-permute-done.3.edge_ref = bf16[8,4096]{1,0:T(8,128)(2,1)S(1)} collective-permute-done((bf16[8,4096]{1,0:T(8,128)(2,1)S(1)}, bf16[8,4096]{1,0:T(8,128)(2,1)S(1)}, u32[]{:S(2)}, u32[]{:S(2)}) %collective-permute-start.3) | collective-permute-done | bytes 65568 | tf_op jit(solution)/shard_map/ppermute | solution.py:225
  39.1 4.9 %collective-permute-done.4 = bf16[4,128,128]{2,1,0:T(8,128)(2,1)S(1)} collective-permute-done((bf16[4,128,128]{2,1,0:T(8,128)(2,1)S(1)}, bf16[4,128,128]{2,1,0:T(8,128)(2,1)S(1)}, u32[]{:S(2)}, u32[]{:S(2)}) %collective-permute-start.4) | collective-permute-done | bytes 131104 | tf_op jit(solution)/shard_map/ppermute | solution.py:225
  44.0 1.4 %gated_product.2.own_ref = bf16[128,2048]{1,0:T(8,128)(2,1)S(1)} custom-call(s32[2]{0:T(128)S(1)} %pad_add_fusion.flags_ref, bf16[128,4096]{1,0:T(8,128)(2,1)S(1)} %copy-done, bf16[128,4096]{1,0:T(8,128)(2,1)S(1)} %copy-done.1, bf16[8,4096]{1,0:T(8,128)(2,1)S(1)} %collective-permute-done.3.edge_ref, bf16[8,192,128]{2,1,0:T(8,128)(2,1)S(1)} %all-to-all-done.1.small_ref), custom_call_target="tpu_custom_call" | custom-call | tf_op jit(solution)/shard_map/gated_product/pallas_call | solution.py:256
  45.5 2.1 %collective-permute-start.5 = (bf16[128,2048]{1,0:T(8,128)(2,1)S(1)}, bf16[128,2048]{1,0:T(8,128)(2,1)S(1)}, u32[]{:S(2)}, u32[]{:S(2)}) collective-permute-start(bf16[128,2048]{1,0:T(8,128)(2,1)S(1)} %gated_product.2.own_ref), channel_id=1, source_target_pairs={{0,1},{1,2},{2,3},{3,4},{4,5},{5,6},{6,7},{7,8},{8,9},{9,10},{10,1... | collective-permute-start | bytes 1572872 | tf_op jit(solution)/shard_map/ppermute | solution.py:225
  47.6 1.4 %gated_product.3.own_ref = bf16[128,2048]{1,0:T(8,128)(2,1)S(1)} custom-call(s32[2]{0:T(128)S(1)} %pad_add_fusion.flags_ref, bf16[128,4096]{1,0:T(8,128)(2,1)S(1)} %copy-done, bf16[128,4096]{1,0:T(8,128)(2,1)S(1)} %copy-done.1, bf16[8,4096]{1,0:T(8,128)(2,1)S(1)} %collective-permute-done.3.edge_ref, bf16[8,192,128]{2,1,0:T(8,128)(2,1)S(1)} %all-to-all-done.1.small_ref), custom_call_target="tpu_custom_call" | custom-call | tf_op jit(solution)/shard_map/gated_product/pallas_call | solution.py:256
  49.1 3.1 %collective-permute-start.6 = (bf16[8,128,128]{2,1,0:T(8,128)(2,1)S(1)}, bf16[8,128,128]{2,1,0:T(8,128)(2,1)S(1)}, u32[]{:S(2)}, u32[]{:S(2)}) collective-permute-start(bf16[8,128,128]{2,1,0:T(8,128)(2,1)S(1)} %slice.3.refs_2_), channel_id=1, source_target_pairs={{0,24},{1,25},{2,26},{3,27},{4,28},{5,29},{6,30},{7,31},{8,0},{9,1... | collective-permute-start | bytes 786440 | tf_op jit(solution)/shard_map/ppermute | solution.py:225
  52.8 1.3 %collective-permute-start.8 = (bf16[8,128,128]{2,1,0:T(8,128)(2,1)S(1)}, bf16[8,128,128]{2,1,0:T(8,128)(2,1)S(1)}, u32[]{:S(2)}, u32[]{:S(2)}) collective-permute-start(bf16[8,128,128]{2,1,0:T(8,128)(2,1)S(1)} %pad_maximum_fusion.1.refs_0_), channel_id=1, source_target_pairs={{8,0},{16,8},{40,32},{48,40},{72,64},{80,72},{104,96},{112,104},{1... | collective-permute-start | bytes 786440 | tf_op jit(solution)/shard_map/ppermute | solution.py:225
  54.1 2.0 %collective-permute-start.12 = (bf16[128,2048]{1,0:T(8,128)(2,1)S(1)}, bf16[128,2048]{1,0:T(8,128)(2,1)S(1)}, u32[]{:S(2)}, u32[]{:S(2)}) collective-permute-start(bf16[128,2048]{1,0:T(8,128)(2,1)S(1)} %gated_product.3.own_ref), channel_id=1, source_target_pairs={{0,1},{1,2},{2,3},{3,4},{4,5},{5,6},{6,7},{7,8},{8,9},{9,10},{10,1... | collective-permute-start | bytes 1572872 | tf_op jit(solution)/shard_map/ppermute | solution.py:225
  56.1 3.8 %collective-permute-done.6.refs_3_ = bf16[8,128,128]{2,1,0:T(8,128)(2,1)S(1)} collective-permute-done((bf16[8,128,128]{2,1,0:T(8,128)(2,1)S(1)}, bf16[8,128,128]{2,1,0:T(8,128)(2,1)S(1)}, u32[]{:S(2)}, u32[]{:S(2)}) %collective-permute-start.6) | collective-permute-done | bytes 262176 | tf_op jit(solution)/shard_map/ppermute | solution.py:225
  59.9 1.3 %collective-permute-start.14 = (bf16[8,128,128]{2,1,0:T(8,128)(2,1)S(1)}, bf16[8,128,128]{2,1,0:T(8,128)(2,1)S(1)}, u32[]{:S(2)}, u32[]{:S(2)}) collective-permute-start(bf16[8,128,128]{2,1,0:T(8,128)(2,1)S(1)} %pad_maximum_fusion.1.refs_0_), channel_id=1, source_target_pairs={{24,0},{56,32},{88,64},{120,96},{152,128},{184,160},{216,192},{248... | collective-permute-start | bytes 786440 | tf_op jit(solution)/shard_map/ppermute | solution.py:225
  61.2 1.7 %collective-permute-done.8.refs_1_ = bf16[8,128,128]{2,1,0:T(8,128)(2,1)S(1)} collective-permute-done((bf16[8,128,128]{2,1,0:T(8,128)(2,1)S(1)}, bf16[8,128,128]{2,1,0:T(8,128)(2,1)S(1)}, u32[]{:S(2)}, u32[]{:S(2)}) %collective-permute-start.8) | collective-permute-done | bytes 262176 | tf_op jit(solution)/shard_map/ppermute | solution.py:225
  62.9 1.3 %collective-permute-start.10 = (bf16[8,128,128]{2,1,0:T(8,128)(2,1)S(1)}, bf16[8,128,128]{2,1,0:T(8,128)(2,1)S(1)}, u32[]{:S(2)}, u32[]{:S(2)}) collective-permute-start(bf16[8,128,128]{2,1,0:T(8,128)(2,1)S(1)} %collective-permute-done.7.refs_5_), channel_id=1, source_target_pairs={{1,0},{9,8},{17,16},{25,24},{33,32},{41,40},{49,48},{57,56},{65,64... | collective-permute-start | bytes 786440 | tf_op jit(solution)/shard_map/ppermute | solution.py:225
  64.2 4.1 %collective-permute-start.9 = (bf16[8,128,128]{2,1,0:T(8,128)(2,1)S(1)}, bf16[8,128,128]{2,1,0:T(8,128)(2,1)S(1)}, u32[]{:S(2)}, u32[]{:S(2)}) collective-permute-start(bf16[8,128,128]{2,1,0:T(8,128)(2,1)S(1)} %collective-permute-done.6.refs_3_), channel_id=1, source_target_pairs={{0,24},{1,25},{2,26},{3,27},{4,28},{5,29},{6,30},{7,31},{8,0},{9,1... | collective-permute-start | bytes 786440 | tf_op jit(solution)/shard_map/ppermute | solution.py:225
  68.3 1.3 %collective-permute-start.13 = (bf16[8,128,128]{2,1,0:T(8,128)(2,1)S(1)}, bf16[8,128,128]{2,1,0:T(8,128)(2,1)S(1)}, u32[]{:S(2)}, u32[]{:S(2)}) collective-permute-start(bf16[8,128,128]{2,1,0:T(8,128)(2,1)S(1)} %collective-permute-done.8.refs_1_), channel_id=1, source_target_pairs={{8,0},{40,32},{72,64},{104,96},{136,128},{168,160},{200,192},{232,... | collective-permute-start | bytes 786440 | tf_op jit(solution)/shard_map/ppermute | solution.py:225
  70.4 3.3 %collective-permute-done.12.halo_ref = bf16[128,2048]{1,0:T(8,128)(2,1)S(1)} collective-permute-done((bf16[128,2048]{1,0:T(8,128)(2,1)S(1)}, bf16[128,2048]{1,0:T(8,128)(2,1)S(1)}, u32[]{:S(2)}, u32[]{:S(2)}) %collective-permute-start.12) | collective-permute-done | bytes 524320 | tf_op jit(solution)/shard_map/ppermute | solution.py:225
  74.6 3.2 %filter_and_gate.2 = bf16[128,2048]{1,0:T(8,128)(2,1)S(1)} custom-call(s32[2]{0:T(128)S(1)} %pad_add_fusion.flags_ref, bf16[128,4096]{1,0:T(8,128)(2,1)S(1)} %copy-done.2, bf16[8,4096]{1,0:T(8,128)(2,1)S(1)} %collective-permute-done.3.edge_ref, bf16[8,192,128]{2,1,0:T(8,128)(2,1)S(1)} %all-to-all-done.1.small_ref, ...), custom_call_target="tpu_custom_call" | custom-call | tf_op jit(solution)/shard_map/filter_and_gate/pallas_call | solution.py:298
  77.9 1.3 %collective-permute-done.14.refs_1_ = bf16[8,128,128]{2,1,0:T(8,128)(2,1)S(1)} collective-permute-done((bf16[8,128,128]{2,1,0:T(8,128)(2,1)S(1)}, bf16[8,128,128]{2,1,0:T(8,128)(2,1)S(1)}, u32[]{:S(2)}, u32[]{:S(2)}) %collective-permute-start.14) | collective-permute-done | bytes 262176 | tf_op jit(solution)/shard_map/ppermute | solution.py:225
  79.2 3.2 %filter_and_gate.3 = bf16[128,2048]{1,0:T(8,128)(2,1)S(1)} custom-call(s32[2]{0:T(128)S(1)} %pad_add_fusion.flags_ref, bf16[128,4096]{1,0:T(8,128)(2,1)S(1)} %copy-done.2, bf16[8,4096]{1,0:T(8,128)(2,1)S(1)} %collective-permute-done.3.edge_ref, bf16[8,192,128]{2,1,0:T(8,128)(2,1)S(1)} %all-to-all-done.1.small_ref, ...), custom_call_target="tpu_custom_call" | custom-call | tf_op jit(solution)/shard_map/filter_and_gate/pallas_call | solution.py:298
  82.5 5.2 %collective-permute-done.11 = bf16[128,2048]{1,0:T(8,128)(2,1)S(1)} collective-permute-done((bf16[128,2048]{1,0:T(8,128)(2,1)S(1)}, bf16[128,2048]{1,0:T(8,128)(2,1)S(1)}, u32[]{:S(2)}, u32[]{:S(2)}) %collective-permute-start.11) | collective-permute-done | bytes 524320 | tf_op jit(solution)/shard_map/ppermute | solution.py:174
  87.7 5.6 %collective-permute-done.15 = bf16[128,2048]{1,0:T(8,128)(2,1)S(1)} collective-permute-done((bf16[128,2048]{1,0:T(8,128)(2,1)S(1)}, bf16[128,2048]{1,0:T(8,128)(2,1)S(1)}, u32[]{:S(2)}, u32[]{:S(2)}) %collective-permute-start.15) | collective-permute-done | bytes 524320 | tf_op jit(solution)/shard_map/ppermute | solution.py:174
  93.3 1.1 %pad_maximum_fusion = bf16[128,4096]{1,0:T(8,128)(2,1)} fusion(bf16[128,2048]{1,0:T(8,128)(2,1)S(1)} %collective-permute-done.15, bf16[128,2048]{1,0:T(8,128)(2,1)S(1)} %collective-permute-done.11), kind=kLoop, calls=%fused_computation | loop fusion | flops 2097152 | bytes 2097152 | tf_op jit(solution)/shard_map/concatenate | solution.py:314
  (29 shorter events, 2.5 us)
Async XLA Ops:
  0.0 44.0 %copy-start = (bf16[128,4096]{1,0:T(8,128)(2,1)S(1)}, bf16[128,4096]{1,0:T(8,128)(2,1)}, u32[]{:S(2)}) copy-start(bf16[128,4096]{1,0:T(8,128)(2,1)} %key_ref.5) | copy-start | bytes 3145732
  0.0 44.0 %copy-start.1 = (bf16[128,4096]{1,0:T(8,128)(2,1)S(1)}, bf16[128,4096]{1,0:T(8,128)(2,1)}, u32[]{:S(2)}) copy-start(bf16[128,4096]{1,0:T(8,128)(2,1)} %value_ref.5) | copy-start | bytes 3145732
  0.0 15.3 %copy-start.5 = (bf16[1,128,128]{2,1,0:T(8,128)(2,1)S(1)}, bf16[1,128,128]{2,1,0:T(8,128)(2,1)}, u32[]{:S(2)}) copy-start(bf16[1,128,128]{2,1,0:T(8,128)(2,1)} %taps_ref.1) | copy-start | bytes 98308
  1.7 8.2 %collective-permute-start = (bf16[1,128,128]{2,1,0:T(8,128)(2,1)S(1)}, bf16[1,128,128]{2,1,0:T(8,128)(2,1)S(1)}, u32[]{:S(2)}, u32[]{:S(2)}) collective-permute-start(bf16[1,128,128]{2,1,0:T(8,128)(2,1)S(1)} %get-tuple-element.22), channel_id=1, source_target_pairs={{1,0},{5,4},{9,8},{13,12},{17,16},{21,20},{25,24},{29,28},{33,32},... | collective-permute-start | bytes 98312 | tf_op jit(solution)/shard_map/ppermute | solution.py:225
  3.0 6.9 %collective-permute-start.1 = (bf16[1,128,128]{2,1,0:T(8,128)(2,1)S(1)}, bf16[1,128,128]{2,1,0:T(8,128)(2,1)S(1)}, u32[]{:S(2)}, u32[]{:S(2)}) collective-permute-start(bf16[1,128,128]{2,1,0:T(8,128)(2,1)S(1)} %get-tuple-element.22), channel_id=1, source_target_pairs={{2,0},{6,4},{10,8},{14,12},{18,16},{22,20},{26,24},{30,28},{34,32}... | collective-permute-start | bytes 98312 | tf_op jit(solution)/shard_map/ppermute | solution.py:225
  4.3 7.9 %collective-permute-start.2 = (bf16[1,128,128]{2,1,0:T(8,128)(2,1)S(1)}, bf16[1,128,128]{2,1,0:T(8,128)(2,1)S(1)}, u32[]{:S(2)}, u32[]{:S(2)}) collective-permute-start(bf16[1,128,128]{2,1,0:T(8,128)(2,1)S(1)} %get-tuple-element.22), channel_id=1, source_target_pairs={{3,0},{7,4},{11,8},{15,12},{19,16},{23,20},{27,24},{31,28},{35,32}... | collective-permute-start | bytes 98312 | tf_op jit(solution)/shard_map/ppermute | solution.py:225
  5.6 9.7 %all-to-all-start = ((bf16[4,16,128]{2,1,0:T(8,128)(2,1)}), bf16[4,16,128]{2,1,0:T(8,128)(2,1)S(1)}, u32[]{:S(2)}, u32[]{:S(2)}) async-start(bf16[4,16,128]{2,1,0:T(8,128)(2,1)} %get-tuple-element.21), calls=%async_computation | async-start | bytes 32768 | tf_op jit(solution)/shard_map/all_to_all | solution.py:178
  16.1 28.0 %all-to-all-start.1 = ((bf16[8,192,128]{2,1,0:T(8,128)(2,1)}), bf16[8,192,128]{2,1,0:T(8,128)(2,1)S(1)}, u32[]{:S(2)}, u32[]{:S(2)}) async-start(bf16[8,192,128]{2,1,0:T(8,128)(2,1)} %spread.1), calls=%async_computation.1 | async-start | bytes 786432 | tf_op jit(solution)/shard_map/all_to_all | solution.py:178
  27.5 16.5 %collective-permute-start.4 = (bf16[4,128,128]{2,1,0:T(8,128)(2,1)S(1)}, bf16[4,128,128]{2,1,0:T(8,128)(2,1)S(1)}, u32[]{:S(2)}, u32[]{:S(2)}) collective-permute-start(bf16[4,128,128]{2,1,0:T(8,128)(2,1)S(1)} %pad_maximum_fusion.2), channel_id=1, source_target_pairs={{4,0},{12,8},{20,16},{28,24},{36,32},{44,40},{52,48},{60,56},{68,6... | collective-permute-start | bytes 393224 | tf_op jit(solution)/shard_map/ppermute | solution.py:225
  28.8 10.3 %collective-permute-start.3 = (bf16[8,4096]{1,0:T(8,128)(2,1)S(1)}, bf16[8,4096]{1,0:T(8,128)(2,1)S(1)}, u32[]{:S(2)}, u32[]{:S(2)}) collective-permute-start(bf16[8,4096]{1,0:T(8,128)(2,1)S(1)} %get-tuple-element.24), channel_id=1, source_target_pairs={{0,1},{1,2},{2,3},{3,4},{4,5},{5,6},{6,7},{7,8},{8,9},{9,10},{10,1... | collective-permute-start | bytes 196616 | tf_op jit(solution)/shard_map/ppermute | solution.py:225
  45.5 24.2 %copy-start.3 = (bf16[512,256]{1,0:T(8,128)(2,1)S(1)}, bf16[512,256]{1,0:T(8,128)(2,1)}, u32[]{:S(2)}) copy-start(bf16[512,256]{1,0:T(8,128)(2,1)} %constant.14.clone.forward_ref.refs_7_) | copy-start | bytes 786436
  45.5 22.8 %collective-permute-start.5 = (bf16[128,2048]{1,0:T(8,128)(2,1)S(1)}, bf16[128,2048]{1,0:T(8,128)(2,1)S(1)}, u32[]{:S(2)}, u32[]{:S(2)}) collective-permute-start(bf16[128,2048]{1,0:T(8,128)(2,1)S(1)} %gated_product.2.own_ref), channel_id=1, source_target_pairs={{0,1},{1,2},{2,3},{3,4},{4,5},{5,6},{6,7},{7,8},{8,9},{9,10},{10,1... | collective-permute-start | bytes 1572872 | tf_op jit(solution)/shard_map/ppermute | solution.py:225
  49.1 10.9 %collective-permute-start.6 = (bf16[8,128,128]{2,1,0:T(8,128)(2,1)S(1)}, bf16[8,128,128]{2,1,0:T(8,128)(2,1)S(1)}, u32[]{:S(2)}, u32[]{:S(2)}) collective-permute-start(bf16[8,128,128]{2,1,0:T(8,128)(2,1)S(1)} %slice.3.refs_2_), channel_id=1, source_target_pairs={{0,24},{1,25},{2,26},{3,27},{4,28},{5,29},{6,30},{7,31},{8,0},{9,1... | collective-permute-start | bytes 786440 | tf_op jit(solution)/shard_map/ppermute | solution.py:225
  52.1 9.1 %collective-permute-start.7 = (bf16[8,128,128]{2,1,0:T(8,128)(2,1)S(1)}, bf16[8,128,128]{2,1,0:T(8,128)(2,1)S(1)}, u32[]{:S(2)}, u32[]{:S(2)}) collective-permute-start(bf16[8,128,128]{2,1,0:T(8,128)(2,1)S(1)} %slice.3.refs_2_), channel_id=1, source_target_pairs={{1,9},{2,10},{3,11},{4,12},{5,13},{6,14},{7,15},{9,17},{10,18},{11... | collective-permute-start | bytes 786440 | tf_op jit(solution)/shard_map/ppermute | solution.py:225
  52.8 10.1 %collective-permute-start.8 = (bf16[8,128,128]{2,1,0:T(8,128)(2,1)S(1)}, bf16[8,128,128]{2,1,0:T(8,128)(2,1)S(1)}, u32[]{:S(2)}, u32[]{:S(2)}) collective-permute-start(bf16[8,128,128]{2,1,0:T(8,128)(2,1)S(1)} %pad_maximum_fusion.1.refs_0_), channel_id=1, source_target_pairs={{8,0},{16,8},{40,32},{48,40},{72,64},{80,72},{104,96},{112,104},{1... | collective-permute-start | bytes 786440 | tf_op jit(solution)/shard_map/ppermute | solution.py:225
  54.1 19.6 %collective-permute-start.12 = (bf16[128,2048]{1,0:T(8,128)(2,1)S(1)}, bf16[128,2048]{1,0:T(8,128)(2,1)S(1)}, u32[]{:S(2)}, u32[]{:S(2)}) collective-permute-start(bf16[128,2048]{1,0:T(8,128)(2,1)S(1)} %gated_product.3.own_ref), channel_id=1, source_target_pairs={{0,1},{1,2},{2,3},{3,4},{4,5},{5,6},{6,7},{7,8},{8,9},{9,10},{10,1... | collective-permute-start | bytes 1572872 | tf_op jit(solution)/shard_map/ppermute | solution.py:225
  59.9 19.3 %collective-permute-start.14 = (bf16[8,128,128]{2,1,0:T(8,128)(2,1)S(1)}, bf16[8,128,128]{2,1,0:T(8,128)(2,1)S(1)}, u32[]{:S(2)}, u32[]{:S(2)}) collective-permute-start(bf16[8,128,128]{2,1,0:T(8,128)(2,1)S(1)} %pad_maximum_fusion.1.refs_0_), channel_id=1, source_target_pairs={{24,0},{56,32},{88,64},{120,96},{152,128},{184,160},{216,192},{248... | collective-permute-start | bytes 786440 | tf_op jit(solution)/shard_map/ppermute | solution.py:225
  62.9 11.4 %collective-permute-start.10 = (bf16[8,128,128]{2,1,0:T(8,128)(2,1)S(1)}, bf16[8,128,128]{2,1,0:T(8,128)(2,1)S(1)}, u32[]{:S(2)}, u32[]{:S(2)}) collective-permute-start(bf16[8,128,128]{2,1,0:T(8,128)(2,1)S(1)} %collective-permute-done.7.refs_5_), channel_id=1, source_target_pairs={{1,0},{9,8},{17,16},{25,24},{33,32},{41,40},{49,48},{57,56},{65,64... | collective-permute-start | bytes 786440 | tf_op jit(solution)/shard_map/ppermute | solution.py:225
  64.2 10.4 %collective-permute-start.9 = (bf16[8,128,128]{2,1,0:T(8,128)(2,1)S(1)}, bf16[8,128,128]{2,1,0:T(8,128)(2,1)S(1)}, u32[]{:S(2)}, u32[]{:S(2)}) collective-permute-start(bf16[8,128,128]{2,1,0:T(8,128)(2,1)S(1)} %collective-permute-done.6.refs_3_), channel_id=1, source_target_pairs={{0,24},{1,25},{2,26},{3,27},{4,28},{5,29},{6,30},{7,31},{8,0},{9,1... | collective-permute-start | bytes 786440 | tf_op jit(solution)/shard_map/ppermute | solution.py:225
  68.3 10.9 %collective-permute-start.13 = (bf16[8,128,128]{2,1,0:T(8,128)(2,1)S(1)}, bf16[8,128,128]{2,1,0:T(8,128)(2,1)S(1)}, u32[]{:S(2)}, u32[]{:S(2)}) collective-permute-start(bf16[8,128,128]{2,1,0:T(8,128)(2,1)S(1)} %collective-permute-done.8.refs_1_), channel_id=1, source_target_pairs={{8,0},{40,32},{72,64},{104,96},{136,128},{168,160},{200,192},{232,... | collective-permute-start | bytes 786440 | tf_op jit(solution)/shard_map/ppermute | solution.py:225
  70.4 4.3 %copy-start.2 = (bf16[128,4096]{1,0:T(8,128)(2,1)S(1)}, bf16[128,4096]{1,0:T(8,128)(2,1)}, u32[]{:S(2)}) copy-start(bf16[128,4096]{1,0:T(8,128)(2,1)} %query_ref.5) | copy-start | bytes 3145732
  70.4 4.3 %copy-start.4 = (bf16[256,256]{1,0:T(8,128)(2,1)S(1)}, bf16[256,256]{1,0:T(8,128)(2,1)}, u32[]{:S(2)}) copy-start(bf16[256,256]{1,0:T(8,128)(2,1)} %constant.15.clone.refs_8_) | copy-start | bytes 393220
  77.9 9.8 %collective-permute-start.11 = (bf16[128,2048]{1,0:T(8,128)(2,1)S(1)}, bf16[128,2048]{1,0:T(8,128)(2,1)S(1)}, u32[]{:S(2)}, u32[]{:S(2)}) collective-permute-start(bf16[128,2048]{1,0:T(8,128)(2,1)S(1)} %filter_and_gate.2), channel_id=1, source_target_pairs={{0,32},{32,64},{64,96},{96,128},{128,160},{160,192},{192,224},{224... | collective-permute-start | bytes 1572872 | tf_op jit(solution)/shard_map/ppermute | solution.py:174
  82.4 10.9 %collective-permute-start.15 = (bf16[128,2048]{1,0:T(8,128)(2,1)S(1)}, bf16[128,2048]{1,0:T(8,128)(2,1)S(1)}, u32[]{:S(2)}, u32[]{:S(2)}) collective-permute-start(bf16[128,2048]{1,0:T(8,128)(2,1)S(1)} %filter_and_gate.3), channel_id=1, source_target_pairs={{0,32},{32,64},{64,96},{96,128},{128,160},{160,192},{192,224},{224... | collective-permute-start | bytes 1572872 | tf_op jit(solution)/shard_map/ppermute | solution.py:174

commit v3 on v2

--- a/solution.py
+++ b/solution.py
@@ -79,11 +79,12 @@
         small_ref[i] = small
 
 
-def spread_kernel(small_ref, taps_ref, out_ref):
+def spread_kernel(small_ref, taps_ref, tail_ref, out_ref):
     for i in range(out_ref.shape[0]):
         out_ref[i, 0:128] = taps_ref[0]
         for x in range(4):
             out_ref[i, 128 + 16 * x : 144 + 16 * x] = small_ref[x]
+        out_ref[i, 192:320] = tail_ref[0]
 
 
 def product_of(key, value, edge, small):
@@ -105,10 +106,10 @@
 
 def choose_taps(flags_ref, blocks, taps_refs, taps_ref):
     index, x = flags_ref[0], flags_ref[1]
-    edge = jnp.where(index & 7 == 0, 1, 0)
+    more = jnp.where(index & 7 == 0, 1, 0)
     for place, block in enumerate(blocks):
         which = (block - x) & 3
-        which = jnp.where(which == 3, 3 + edge, which)
+        which = jnp.where(which == 3, which + more, which)
         for step, ref in enumerate(taps_refs):
 
             @pl.when(which == step)
@@ -230,26 +231,18 @@
     def shift_x(value, steps):
         return lax.ppermute(value, "ctx_x", [(i, (i + steps) % n_x) for i in range(n_x)])
 
-    def send_z(value, step, stops):
-        return send(value, [(x * n_z + z + step, x * n_z + z) for x in range(n_x) for z in stops])
-
     edge = shift(edge_own, 1)
     along_x = exchange(small_own, "ctx_x")
-    tails = [tail] + [send_z(tail, step, (0, 4)) for step in (1, 2, 3)]
-    tail = jnp.concatenate(tails, axis=0)
-    along_x, tail = lax.optimization_barrier((along_x, tail))
     spread = pl.pallas_call(
         spread_kernel,
-        in_specs=[vmem, vmem],
+        in_specs=[vmem] * 3,
         out_specs=vmem,
-        out_shape=jax.ShapeDtypeStruct((n_z, 192, 128), BF),
+        out_shape=jax.ShapeDtypeStruct((n_z, 320, 128), BF),
         compiler_params=params,
         name="spread",
-    )(along_x, long_taps)
+    )(along_x, long_taps, tail)
     along_z = exchange(spread, "ctx_z")
-    last_tail = send_z(tail, 4, (0,))
-    along_z, edge, tail, last_tail = lax.optimization_barrier((along_z, edge, tail, last_tail))
-    tail = jnp.concatenate([tail, last_tail], axis=0)
+    along_z, edge = lax.optimization_barrier((along_z, edge))
 
     products, halos = [], []
     for blocks in BLOCKS:
@@ -264,21 +257,28 @@
         products.append(product)
         halos.append(shift(product, 1))
 
-    taps, tail, *products = lax.optimization_barrier((along_z, tail, *products))
-    taps = taps[:, 0:128]
-    inner = [(x * n_z + z, (x + 1) % n_x * n_z + z) for x in range(n_x) for z in range(1, n_z)]
-    taps_before = send(taps, inner)
-    taps_after = send(taps, [(i, (i - n_z) % n_ctx) for i in range(n_ctx)])
+    wide, *products = lax.optimization_barrier((along_z, *products))
+    taps = wide[:, 0:128]
+    tail = wide[:, 192:320]
+
+    def send_x(value, steps, first_z):
+        pairs = [
+            (x * n_z + z, (x + steps) % n_x * n_z + z) for x in range(n_x) for z in range(first_z, n_z)
+        ]
+        return send(value, pairs)
+
+    def down(value):
+        return send(value, [(x * n_z + 1, x * n_z) for x in range(n_x)])
+
+    taps_after = send_x(taps, -1, 0)
+    taps_before = send_x(taps, 1, 1)
     prior_one = send(tail, [(n_z, 0), (2 * n_z, n_z)])
     prior_three = send(tail, [(3 * n_z, 0)])
     taps_after, taps_before, prior_one = lax.optimization_barrier(
         (taps_after, taps_before, prior_one)
     )
-    taps_two = send(taps_after, [(i, (i - n_z) % n_ctx) for i in range(n_ctx)])
-    taps_first = send(taps_before, [(x * n_z + 1, x * n_z) for x in range(n_x)])
-    prior_two = send(prior_one, [(n_z, 0)])
-    all_taps = [taps, taps_after, taps_two, taps_before, taps_first]
-    priors = [tail, prior_one, prior_two, prior_three]
+    all_taps = [taps, taps_after, send_x(taps_after, -1, 0), taps_before, down(taps_before)]
+    priors = [tail, prior_one, send(prior_one, [(n_z, 0)]), prior_three]
 
     forward, inverse = dft_matrices()
     handed = []

time: 95 us -> 92.7 us (0.976)
  blocking collectives: 0 us -> 9.46 us
  starting transfers between devices: 41.3 us -> 34 us
  waiting for transfers between devices: 38.3 us -> 34.5 us
    all_to_all x0 -> x1, blocking collectives: none -> 9.46 us  [exchange(): return lax.all_to_all(copies, axis, split_axis=0, concat_axis=0, tiled=True)]
    all_to_all x2 -> x1, starting transfers between devices: 15.8 us -> 10.3 us  [exchange(): return lax.all_to_all(copies, axis, split_axis=0, concat_axis=0, tiled=True)]
    ppermute x14 -> x10, waiting for transfers between devices: 24.4 us -> 20.2 us  [send(): return lax.ppermute(value, ctx, pairs)]
    ppermute x14 -> x10, starting transfers between devices: 25.5 us -> 22.9 us  [send(): return lax.ppermute(value, ctx, pairs)]
    all_to_all x2 -> x1, waiting for transfers between devices: 3.05 us -> 3.63 us  [exchange(): return lax.all_to_all(copies, axis, split_axis=0, concat_axis=0, tiled=True)]
  transfers between devices with their start and end apart: 18 -> 13, of which waited for: 11 -> 8; matrix products, arithmetic and copies ran while one was open for 0% -> 0% of each run, Pallas kernels for 10% -> 10%
where the time goes in v3:
time: 92.7 us; the launch traced here: 92.2 us
  waiting for transfers between devices  34.5 us (37%)
  starting transfers between devices  34 us (37%)
  Pallas kernels  12.9 us (14%)
  blocking collectives  9.46 us (10%)
  other arithmetic  1.14 us (1%)
    ppermute x10, starting transfers between devices, send(): return lax.ppermute(value, ctx, pairs)  22.9 us
    ppermute x10, waiting for transfers between devices, send(): return lax.ppermute(value, ctx, pairs)  20.2 us
    ppermute x2, waiting for transfers between devices, shift_by_one(): lax.ppermute(value, axes, [(i, (i + 1) % count) for i in range(count)])  10.6 us
    all_to_all x1, starting transfers between devices, exchange(): return lax.all_to_all(copies, axis, split_axis=0, concat_axis=0, tiled=True)  10.3 us
    all_to_all x1, blocking collectives, exchange(): return lax.all_to_all(copies, axis, split_axis=0, concat_axis=0, tiled=True)  9.46 us
    pallas_call x2, Pallas kernels, body(): pl.pallas_call(functools.partial(filter_kernel, blocks), in_specs=[smem]...  6.49 us
    all_to_all x1, waiting for transfers between devices, exchange(): return lax.all_to_all(copies, axis, split_axis=0, concat_axis=0, tiled=True)  3.63 us
    pallas_call x2, Pallas kernels, body(): pl.pallas_call(functools.partial(product_kernel, blocks), in_specs=[smem]...  2.87 us
  transfers between devices with their start and end apart: 13, of which 8 were waited for; matrix products, arithmetic and copies ran while one was open for 0% of the time, Pallas kernels for 10%

profile of v3, /device:TPU:32, one launch (start us, length us, event | category | flops | bytes accessed | tf_op | source)
XLA Modules:
  0.0 92.2 jit_solution(10968005632941666979)
XLA Ops:
  0.0 1.2 %prepare.1 = (bf16[8,4096]{1,0:T(8,128)(2,1)S(1)}, bf16[4,16,128]{2,1,0:T(8,128)(2,1)S(1)}, bf16[1,128,128]{2,1,0:T(8,128)(2,1)S(1)}) custom-call(bf16[128,4096]{1,0:T(8,128)(2,1)} %query_ref.5, bf16[128,4096]{1,0:T(8,128)(2,1)} %key_ref.5, bf16[128,4096]{1,0:T(8,128)(2,1)} %value_ref.5, bf16[1,3,3,128]{3,2,1,0:T(4,128)(2,1)} %short_ref.1, ...), custom_call_target="tpu_custom_call" | custom-call | tf_op jit(solution)/shard_map/prepare/pallas_call | solution.py:204
  1.2 9.5 %all_to_all.10.small_ref = bf16[4,16,128]{2,1,0:T(8,128)(2,1)S(1)} all-to-all(bf16[4,16,128]{2,1,0:T(8,128)(2,1)S(1)} %get-tuple-element.16), channel_id=1, replica_groups=mesh['section'=16,'ctx_x'=4,'ctx_z'=8] {'ctx_x'}, dimensions={0} | all-to-all | bytes 32768 | tf_op jit(solution)/shard_map/all_to_all | solution.py:179
  10.6 0.9 spread.1
  11.5 10.3 %all-to-all-start.1 = ((bf16[8,320,128]{2,1,0:T(8,128)(2,1)}), bf16[8,320,128]{2,1,0:T(8,128)(2,1)S(1)}, u32[]{:S(2)}, u32[]{:S(2)}) async-start(bf16[8,320,128]{2,1,0:T(8,128)(2,1)} %spread.1), calls=%async_computation.1 | async-start | bytes 1310720 | tf_op jit(solution)/shard_map/all_to_all | solution.py:179
  21.9 3.9 %collective-permute-start = (bf16[8,4096]{1,0:T(8,128)(2,1)S(1)}, bf16[8,4096]{1,0:T(8,128)(2,1)S(1)}, u32[]{:S(2)}, u32[]{:S(2)}) collective-permute-start(bf16[8,4096]{1,0:T(8,128)(2,1)S(1)} %get-tuple-element.18), channel_id=1, source_target_pairs={{0,1},{1,2},{2,3},{3,4},{4,5},{5,6},{6,7},{7,8},{8,9},{9,10},{10,1... | collective-permute-start | bytes 196616 | tf_op jit(solution)/shard_map/ppermute | solution.py:226
  25.8 0.1 pad_add_fusion.flags_ref
  25.9 12.0 %collective-permute-done.edge_ref = bf16[8,4096]{1,0:T(8,128)(2,1)S(1)} collective-permute-done((bf16[8,4096]{1,0:T(8,128)(2,1)S(1)}, bf16[8,4096]{1,0:T(8,128)(2,1)S(1)}, u32[]{:S(2)}, u32[]{:S(2)}) %collective-permute-start) | collective-permute-done | bytes 65568 | tf_op jit(solution)/shard_map/ppermute | solution.py:226
  37.8 3.6 %all-to-all-done.1.small_ref = bf16[8,320,128]{2,1,0:T(8,128)(2,1)S(1)} async-done(((bf16[8,320,128]{2,1,0:T(8,128)(2,1)}), bf16[8,320,128]{2,1,0:T(8,128)(2,1)S(1)}, u32[]{:S(2)}, u32[]{:S(2)}) %all-to-all-start.1) | async-done | bytes 655392 | tf_op jit(solution)/shard_map/all_to_all | solution.py:179
  41.5 1.4 %gated_product.2.own_ref = bf16[128,2048]{1,0:T(8,128)(2,1)S(1)} custom-call(s32[2]{0:T(128)S(1)} %pad_add_fusion.flags_ref, bf16[128,4096]{1,0:T(8,128)(2,1)S(1)} %copy-done.1, bf16[128,4096]{1,0:T(8,128)(2,1)S(1)} %copy-done.2, bf16[8,4096]{1,0:T(8,128)(2,1)S(1)} %collective-permute-done.edge_ref, bf16[8,320,128]{2,1,0:T(8,128)(2,1)S(1)} %all-to-all-done.1.small_ref), custom_call_target="tpu_custom_call" | custom-call | tf_op jit(solution)/shard_map/gated_product/pallas_call | solution.py:249
  42.9 2.1 %collective-permute-start.1 = (bf16[128,2048]{1,0:T(8,128)(2,1)S(1)}, bf16[128,2048]{1,0:T(8,128)(2,1)S(1)}, u32[]{:S(2)}, u32[]{:S(2)}) collective-permute-start(bf16[128,2048]{1,0:T(8,128)(2,1)S(1)} %gated_product.2.own_ref), channel_id=1, source_target_pairs={{0,1},{1,2},{2,3},{3,4},{4,5},{5,6},{6,7},{7,8},{8,9},{9,10},{10,1... | collective-permute-start | bytes 1572872 | tf_op jit(solution)/shard_map/ppermute | solution.py:226
  45.0 1.4 %gated_product.3.own_ref = bf16[128,2048]{1,0:T(8,128)(2,1)S(1)} custom-call(s32[2]{0:T(128)S(1)} %pad_add_fusion.flags_ref, bf16[128,4096]{1,0:T(8,128)(2,1)S(1)} %copy-done.1, bf16[128,4096]{1,0:T(8,128)(2,1)S(1)} %copy-done.2, bf16[8,4096]{1,0:T(8,128)(2,1)S(1)} %collective-permute-done.edge_ref, bf16[8,320,128]{2,1,0:T(8,128)(2,1)S(1)} %all-to-all-done.1.small_ref), custom_call_target="tpu_custom_call" | custom-call | tf_op jit(solution)/shard_map/gated_product/pallas_call | solution.py:249
  46.5 3.1 %collective-permute-start.2 = (bf16[8,128,128]{2,1,0:T(8,128)(2,1)S(1)}, bf16[8,128,128]{2,1,0:T(8,128)(2,1)S(1)}, u32[]{:S(2)}, u32[]{:S(2)}) collective-permute-start(bf16[8,128,128]{2,1,0:T(8,128)(2,1)S(1)} %get-tuple-element.28.refs_2_), channel_id=1, source_target_pairs={{0,24},{1,25},{2,26},{3,27},{4,28},{5,29},{6,30},{7,31},{8,0},{9,1... | collective-permute-start | bytes 786440 | tf_op jit(solution)/shard_map/ppermute | solution.py:226
  49.6 0.7 collective-permute-start.3
  50.3 1.4 %collective-permute-start.4 = (bf16[8,128,128]{2,1,0:T(8,128)(2,1)S(1)}, bf16[8,128,128]{2,1,0:T(8,128)(2,1)S(1)}, u32[]{:S(2)}, u32[]{:S(2)}) collective-permute-start(bf16[8,128,128]{2,1,0:T(8,128)(2,1)S(1)} %get-tuple-element.27.refs_0_), channel_id=1, source_target_pairs={{8,0},{16,8},{40,32},{48,40},{72,64},{80,72},{104,96},{112,104},{1... | collective-permute-start | bytes 786440 | tf_op jit(solution)/shard_map/ppermute | solution.py:226
  51.7 3.6 %collective-permute-start.8 = (bf16[128,2048]{1,0:T(8,128)(2,1)S(1)}, bf16[128,2048]{1,0:T(8,128)(2,1)S(1)}, u32[]{:S(2)}, u32[]{:S(2)}) collective-permute-start(bf16[128,2048]{1,0:T(8,128)(2,1)S(1)} %gated_product.3.own_ref), channel_id=1, source_target_pairs={{0,1},{1,2},{2,3},{3,4},{4,5},{5,6},{6,7},{7,8},{8,9},{9,10},{10,1... | collective-permute-start | bytes 1572872 | tf_op jit(solution)/shard_map/ppermute | solution.py:226
  55.3 1.8 %collective-permute-done.2.refs_3_ = bf16[8,128,128]{2,1,0:T(8,128)(2,1)S(1)} collective-permute-done((bf16[8,128,128]{2,1,0:T(8,128)(2,1)S(1)}, bf16[8,128,128]{2,1,0:T(8,128)(2,1)S(1)}, u32[]{:S(2)}, u32[]{:S(2)}) %collective-permute-start.2) | collective-permute-done | bytes 262176 | tf_op jit(solution)/shard_map/ppermute | solution.py:226
  57.1 1.3 %collective-permute-start.10 = (bf16[8,128,128]{2,1,0:T(8,128)(2,1)S(1)}, bf16[8,128,128]{2,1,0:T(8,128)(2,1)S(1)}, u32[]{:S(2)}, u32[]{:S(2)}) collective-permute-start(bf16[8,128,128]{2,1,0:T(8,128)(2,1)S(1)} %get-tuple-element.27.refs_0_), channel_id=1, source_target_pairs={{24,0},{56,32},{88,64},{120,96},{152,128},{184,160},{216,192},{248... | collective-permute-start | bytes 786440 | tf_op jit(solution)/shard_map/ppermute | solution.py:226
  58.4 1.5 %collective-permute-done.4.refs_1_ = bf16[8,128,128]{2,1,0:T(8,128)(2,1)S(1)} collective-permute-done((bf16[8,128,128]{2,1,0:T(8,128)(2,1)S(1)}, bf16[8,128,128]{2,1,0:T(8,128)(2,1)S(1)}, u32[]{:S(2)}, u32[]{:S(2)}) %collective-permute-start.4) | collective-permute-done | bytes 262176 | tf_op jit(solution)/shard_map/ppermute | solution.py:226
  59.9 4.3 %collective-permute-start.5 = (bf16[8,128,128]{2,1,0:T(8,128)(2,1)S(1)}, bf16[8,128,128]{2,1,0:T(8,128)(2,1)S(1)}, u32[]{:S(2)}, u32[]{:S(2)}) collective-permute-start(bf16[8,128,128]{2,1,0:T(8,128)(2,1)S(1)} %collective-permute-done.2.refs_3_), channel_id=1, source_target_pairs={{0,24},{1,25},{2,26},{3,27},{4,28},{5,29},{6,30},{7,31},{8,0},{9,1... | collective-permute-start | bytes 786440 | tf_op jit(solution)/shard_map/ppermute | solution.py:226
  64.2 1.3 %collective-permute-start.6 = (bf16[8,128,128]{2,1,0:T(8,128)(2,1)S(1)}, bf16[8,128,128]{2,1,0:T(8,128)(2,1)S(1)}, u32[]{:S(2)}, u32[]{:S(2)}) collective-permute-start(bf16[8,128,128]{2,1,0:T(8,128)(2,1)S(1)} %collective-permute-done.3.refs_5_), channel_id=1, source_target_pairs={{1,0},{9,8},{17,16},{25,24},{33,32},{41,40},{49,48},{57,56},{65,64... | collective-permute-start | bytes 786440 | tf_op jit(solution)/shard_map/ppermute | solution.py:226
  65.5 1.3 %collective-permute-start.9 = (bf16[8,128,128]{2,1,0:T(8,128)(2,1)S(1)}, bf16[8,128,128]{2,1,0:T(8,128)(2,1)S(1)}, u32[]{:S(2)}, u32[]{:S(2)}) collective-permute-start(bf16[8,128,128]{2,1,0:T(8,128)(2,1)S(1)} %collective-permute-done.4.refs_1_), channel_id=1, source_target_pairs={{8,0},{40,32},{72,64},{104,96},{136,128},{168,160},{200,192},{232,... | collective-permute-start | bytes 786440 | tf_op jit(solution)/shard_map/ppermute | solution.py:226
  66.8 0.7 product_spectrum.2.spec_ref
  67.5 2.6 %collective-permute-done.5.refs_4_ = bf16[8,128,128]{2,1,0:T(8,128)(2,1)S(1)} collective-permute-done((bf16[8,128,128]{2,1,0:T(8,128)(2,1)S(1)}, bf16[8,128,128]{2,1,0:T(8,128)(2,1)S(1)}, u32[]{:S(2)}, u32[]{:S(2)}) %collective-permute-start.5) | collective-permute-done | bytes 262176 | tf_op jit(solution)/shard_map/ppermute | solution.py:226
  70.1 2.3 %collective-permute-done.6.refs_6_ = bf16[8,128,128]{2,1,0:T(8,128)(2,1)S(1)} collective-permute-done((bf16[8,128,128]{2,1,0:T(8,128)(2,1)S(1)}, bf16[8,128,128]{2,1,0:T(8,128)(2,1)S(1)}, u32[]{:S(2)}, u32[]{:S(2)}) %collective-permute-start.6) | collective-permute-done | bytes 262176 | tf_op jit(solution)/shard_map/ppermute | solution.py:226
  72.5 3.2 %filter_and_gate.2 = bf16[128,2048]{1,0:T(8,128)(2,1)S(1)} custom-call(s32[2]{0:T(128)S(1)} %pad_add_fusion.flags_ref, bf16[128,4096]{1,0:T(8,128)(2,1)S(1)} %copy-done, bf16[8,4096]{1,0:T(8,128)(2,1)S(1)} %collective-permute-done.edge_ref, bf16[8,320,128]{2,1,0:T(8,128)(2,1)S(1)} %all-to-all-done.1.small_ref, bf16[128,2048]{1,0:T(8,128)(2,1)S(1)} %gated_product.2.own_ref, ...), custom_call_target="tpu_custom_call" | custom-call | tf_op jit(solution)/shard_map/filter_and_gate/pallas_call | solution.py:298
  75.7 0.0 collective-permute-start.7
  75.7 0.7 product_spectrum.3.spec_ref
  76.5 3.2 %filter_and_gate.3 = bf16[128,2048]{1,0:T(8,128)(2,1)S(1)} custom-call(s32[2]{0:T(128)S(1)} %pad_add_fusion.flags_ref, bf16[128,4096]{1,0:T(8,128)(2,1)S(1)} %copy-done, bf16[8,4096]{1,0:T(8,128)(2,1)S(1)} %collective-permute-done.edge_ref, bf16[8,320,128]{2,1,0:T(8,128)(2,1)S(1)} %all-to-all-done.1.small_ref, bf16[128,2048]{1,0:T(8,128)(2,1)S(1)} %gated_product.3.own_ref, ...), custom_call_target="tpu_custom_call" | custom-call | tf_op jit(solution)/shard_map/filter_and_gate/pallas_call | solution.py:298
  79.7 0.8 collective-permute-start.11
  80.5 5.0 %collective-permute-done.7 = bf16[128,2048]{1,0:T(8,128)(2,1)S(1)} collective-permute-done((bf16[128,2048]{1,0:T(8,128)(2,1)S(1)}, bf16[128,2048]{1,0:T(8,128)(2,1)S(1)}, u32[]{:S(2)}, u32[]{:S(2)}) %collective-permute-start.7) | collective-permute-done | bytes 524320 | tf_op jit(solution)/shard_map/ppermute | solution.py:175
  85.5 5.6 %collective-permute-done.11 = bf16[128,2048]{1,0:T(8,128)(2,1)S(1)} collective-permute-done((bf16[128,2048]{1,0:T(8,128)(2,1)S(1)}, bf16[128,2048]{1,0:T(8,128)(2,1)S(1)}, u32[]{:S(2)}, u32[]{:S(2)}) %collective-permute-start.11) | collective-permute-done | bytes 524320 | tf_op jit(solution)/shard_map/ppermute | solution.py:175
  91.2 1.1 %pad_maximum_fusion = bf16[128,4096]{1,0:T(8,128)(2,1)} fusion(bf16[128,2048]{1,0:T(8,128)(2,1)S(1)} %collective-permute-done.11, bf16[128,2048]{1,0:T(8,128)(2,1)S(1)} %collective-permute-done.7), kind=kLoop, calls=%fused_computation | loop fusion | flops 2097152 | bytes 2097152 | tf_op jit(solution)/shard_map/concatenate | solution.py:314
  (18 shorter events, 0.1 us)
Async XLA Ops:
  0.0 41.5 %copy-start.1 = (bf16[128,4096]{1,0:T(8,128)(2,1)S(1)}, bf16[128,4096]{1,0:T(8,128)(2,1)}, u32[]{:S(2)}) copy-start(bf16[128,4096]{1,0:T(8,128)(2,1)} %key_ref.5) | copy-start | bytes 3145732
  0.0 41.5 %copy-start.2 = (bf16[128,4096]{1,0:T(8,128)(2,1)S(1)}, bf16[128,4096]{1,0:T(8,128)(2,1)}, u32[]{:S(2)}) copy-start(bf16[128,4096]{1,0:T(8,128)(2,1)} %value_ref.5) | copy-start | bytes 3145732
  0.0 10.6 %copy-start.5 = (bf16[1,128,128]{2,1,0:T(8,128)(2,1)S(1)}, bf16[1,128,128]{2,1,0:T(8,128)(2,1)}, u32[]{:S(2)}) copy-start(bf16[1,128,128]{2,1,0:T(8,128)(2,1)} %taps_ref.1) | copy-start | bytes 98308
  11.5 29.9 %all-to-all-start.1 = ((bf16[8,320,128]{2,1,0:T(8,128)(2,1)}), bf16[8,320,128]{2,1,0:T(8,128)(2,1)S(1)}, u32[]{:S(2)}, u32[]{:S(2)}) async-start(bf16[8,320,128]{2,1,0:T(8,128)(2,1)} %spread.1), calls=%async_computation.1 | async-start | bytes 1310720 | tf_op jit(solution)/shard_map/all_to_all | solution.py:179
  21.9 16.0 %collective-permute-start = (bf16[8,4096]{1,0:T(8,128)(2,1)S(1)}, bf16[8,4096]{1,0:T(8,128)(2,1)S(1)}, u32[]{:S(2)}, u32[]{:S(2)}) collective-permute-start(bf16[8,4096]{1,0:T(8,128)(2,1)S(1)} %get-tuple-element.18), channel_id=1, source_target_pairs={{0,1},{1,2},{2,3},{3,4},{4,5},{5,6},{6,7},{7,8},{8,9},{9,10},{10,1... | collective-permute-start | bytes 196616 | tf_op jit(solution)/shard_map/ppermute | solution.py:226
  42.9 23.9 %copy-start.3 = (bf16[512,256]{1,0:T(8,128)(2,1)S(1)}, bf16[512,256]{1,0:T(8,128)(2,1)}, u32[]{:S(2)}) copy-start(bf16[512,256]{1,0:T(8,128)(2,1)} %constant.14.clone.forward_ref.refs_7_) | copy-start | bytes 786436
  42.9 22.5 %collective-permute-start.1 = (bf16[128,2048]{1,0:T(8,128)(2,1)S(1)}, bf16[128,2048]{1,0:T(8,128)(2,1)S(1)}, u32[]{:S(2)}, u32[]{:S(2)}) collective-permute-start(bf16[128,2048]{1,0:T(8,128)(2,1)S(1)} %gated_product.2.own_ref), channel_id=1, source_target_pairs={{0,1},{1,2},{2,3},{3,4},{4,5},{5,6},{6,7},{7,8},{8,9},{9,10},{10,1... | collective-permute-start | bytes 1572872 | tf_op jit(solution)/shard_map/ppermute | solution.py:226
  46.5 10.6 %collective-permute-start.2 = (bf16[8,128,128]{2,1,0:T(8,128)(2,1)S(1)}, bf16[8,128,128]{2,1,0:T(8,128)(2,1)S(1)}, u32[]{:S(2)}, u32[]{:S(2)}) collective-permute-start(bf16[8,128,128]{2,1,0:T(8,128)(2,1)S(1)} %get-tuple-element.28.refs_2_), channel_id=1, source_target_pairs={{0,24},{1,25},{2,26},{3,27},{4,28},{5,29},{6,30},{7,31},{8,0},{9,1... | collective-permute-start | bytes 786440 | tf_op jit(solution)/shard_map/ppermute | solution.py:226
  49.6 8.8 %collective-permute-start.3 = (bf16[8,128,128]{2,1,0:T(8,128)(2,1)S(1)}, bf16[8,128,128]{2,1,0:T(8,128)(2,1)S(1)}, u32[]{:S(2)}, u32[]{:S(2)}) collective-permute-start(bf16[8,128,128]{2,1,0:T(8,128)(2,1)S(1)} %get-tuple-element.28.refs_2_), channel_id=1, source_target_pairs={{1,9},{2,10},{3,11},{4,12},{5,13},{6,14},{7,15},{9,17},{10,18},{11... | collective-permute-start | bytes 786440 | tf_op jit(solution)/shard_map/ppermute | solution.py:226
  50.3 22.2 %copy-start = (bf16[128,4096]{1,0:T(8,128)(2,1)S(1)}, bf16[128,4096]{1,0:T(8,128)(2,1)}, u32[]{:S(2)}) copy-start(bf16[128,4096]{1,0:T(8,128)(2,1)} %query_ref.5) | copy-start | bytes 3145732
  50.3 22.2 %copy-start.4 = (bf16[256,256]{1,0:T(8,128)(2,1)S(1)}, bf16[256,256]{1,0:T(8,128)(2,1)}, u32[]{:S(2)}) copy-start(bf16[256,256]{1,0:T(8,128)(2,1)} %constant.15.clone.refs_8_) | copy-start | bytes 393220
  50.3 9.6 %collective-permute-start.4 = (bf16[8,128,128]{2,1,0:T(8,128)(2,1)S(1)}, bf16[8,128,128]{2,1,0:T(8,128)(2,1)S(1)}, u32[]{:S(2)}, u32[]{:S(2)}) collective-permute-start(bf16[8,128,128]{2,1,0:T(8,128)(2,1)S(1)} %get-tuple-element.27.refs_0_), channel_id=1, source_target_pairs={{8,0},{16,8},{40,32},{48,40},{72,64},{80,72},{104,96},{112,104},{1... | collective-permute-start | bytes 786440 | tf_op jit(solution)/shard_map/ppermute | solution.py:226
  51.7 24.0 %collective-permute-start.8 = (bf16[128,2048]{1,0:T(8,128)(2,1)S(1)}, bf16[128,2048]{1,0:T(8,128)(2,1)S(1)}, u32[]{:S(2)}, u32[]{:S(2)}) collective-permute-start(bf16[128,2048]{1,0:T(8,128)(2,1)S(1)} %gated_product.3.own_ref), channel_id=1, source_target_pairs={{0,1},{1,2},{2,3},{3,4},{4,5},{5,6},{6,7},{7,8},{8,9},{9,10},{10,1... | collective-permute-start | bytes 1572872 | tf_op jit(solution)/shard_map/ppermute | solution.py:226
  57.1 19.4 %collective-permute-start.10 = (bf16[8,128,128]{2,1,0:T(8,128)(2,1)S(1)}, bf16[8,128,128]{2,1,0:T(8,128)(2,1)S(1)}, u32[]{:S(2)}, u32[]{:S(2)}) collective-permute-start(bf16[8,128,128]{2,1,0:T(8,128)(2,1)S(1)} %get-tuple-element.27.refs_0_), channel_id=1, source_target_pairs={{24,0},{56,32},{88,64},{120,96},{152,128},{184,160},{216,192},{248... | collective-permute-start | bytes 786440 | tf_op jit(solution)/shard_map/ppermute | solution.py:226
  59.9 10.2 %collective-permute-start.5 = (bf16[8,128,128]{2,1,0:T(8,128)(2,1)S(1)}, bf16[8,128,128]{2,1,0:T(8,128)(2,1)S(1)}, u32[]{:S(2)}, u32[]{:S(2)}) collective-permute-start(bf16[8,128,128]{2,1,0:T(8,128)(2,1)S(1)} %collective-permute-done.2.refs_3_), channel_id=1, source_target_pairs={{0,24},{1,25},{2,26},{3,27},{4,28},{5,29},{6,30},{7,31},{8,0},{9,1... | collective-permute-start | bytes 786440 | tf_op jit(solution)/shard_map/ppermute | solution.py:226
  64.2 8.3 %collective-permute-start.6 = (bf16[8,128,128]{2,1,0:T(8,128)(2,1)S(1)}, bf16[8,128,128]{2,1,0:T(8,128)(2,1)S(1)}, u32[]{:S(2)}, u32[]{:S(2)}) collective-permute-start(bf16[8,128,128]{2,1,0:T(8,128)(2,1)S(1)} %collective-permute-done.3.refs_5_), channel_id=1, source_target_pairs={{1,0},{9,8},{17,16},{25,24},{33,32},{41,40},{49,48},{57,56},{65,64... | collective-permute-start | bytes 786440 | tf_op jit(solution)/shard_map/ppermute | solution.py:226
  65.5 11.0 %collective-permute-start.9 = (bf16[8,128,128]{2,1,0:T(8,128)(2,1)S(1)}, bf16[8,128,128]{2,1,0:T(8,128)(2,1)S(1)}, u32[]{:S(2)}, u32[]{:S(2)}) collective-permute-start(bf16[8,128,128]{2,1,0:T(8,128)(2,1)S(1)} %collective-permute-done.4.refs_1_), channel_id=1, source_target_pairs={{8,0},{40,32},{72,64},{104,96},{136,128},{168,160},{200,192},{232,... | collective-permute-start | bytes 786440 | tf_op jit(solution)/shard_map/ppermute | solution.py:226
  75.7 9.8 %collective-permute-start.7 = (bf16[128,2048]{1,0:T(8,128)(2,1)S(1)}, bf16[128,2048]{1,0:T(8,128)(2,1)S(1)}, u32[]{:S(2)}, u32[]{:S(2)}) collective-permute-start(bf16[128,2048]{1,0:T(8,128)(2,1)S(1)} %filter_and_gate.2), channel_id=1, source_target_pairs={{0,32},{32,64},{64,96},{96,128},{128,160},{160,192},{192,224},{224... | collective-permute-start | bytes 1572872 | tf_op jit(solution)/shard_map/ppermute | solution.py:175
  79.7 11.4 %collective-permute-start.11 = (bf16[128,2048]{1,0:T(8,128)(2,1)S(1)}, bf16[128,2048]{1,0:T(8,128)(2,1)S(1)}, u32[]{:S(2)}, u32[]{:S(2)}) collective-permute-start(bf16[128,2048]{1,0:T(8,128)(2,1)S(1)} %filter_and_gate.3), channel_id=1, source_target_pairs={{0,32},{32,64},{64,96},{96,128},{128,160},{160,192},{192,224},{224... | collective-permute-start | bytes 1572872 | tf_op jit(solution)/shard_map/ppermute | solution.py:175

commit v4 on v3

--- a/solution.py
+++ b/solution.py
@@ -129,7 +129,7 @@
         out_ref[:, here] = spectrum_of(halo_ref[:, here], own_ref[:, here], forward_ref)
 
 
-def filter_kernel(blocks, flags_ref, query_ref, edge_ref, small_ref, own_ref, spec_ref, *refs):
+def filter_kernel(blocks, offset, flags_ref, query_ref, edge_ref, small_ref, own_ref, spec_ref, *refs):
     prior_refs, refs = refs[: len(blocks)], refs[len(blocks) :]
     taps_refs, (forward_ref, inverse_ref, out_ref, taps_ref, both_ref) = refs[:5], refs[5:]
     first = flags_ref[0] == 0
@@ -143,11 +143,13 @@
                 place, z = divmod(s * STEP // 128 + i, 8)
                 prior.append(prior_refs[place][z])
             prior = jnp.concatenate(prior, axis=1)
-            both_ref[:, here] = spectrum_of(prior, own_ref[:, here], forward_ref)
+            both_ref[:, here] = spectrum_of(
+                prior, own_ref[:, pl.ds(offset + s * STEP, STEP)], forward_ref
+            )
 
     @pl.when(jnp.logical_not(first))
     def _():
-        both_ref[...] = spec_ref[...]
+        both_ref[...] = spec_ref[:, pl.ds(offset, out_ref.shape[1])]
 
     choose_taps(flags_ref, blocks, taps_refs, taps_ref)
     groups = STEP // 128
@@ -167,7 +169,7 @@
         y_lo = (spec_y - y_hi.astype(F32)).astype(BF)
         both = dot(inverse_ref[...], y_hi)
         filtered = both[:128] + both[128:] + dot(inverse_ref[0:128, :], y_lo)
-        own = own_ref[:, here].astype(F32)
+        own = own_ref[:, pl.ds(offset + s * STEP, STEP)].astype(F32)
         out_ref[:, here] = (query * (filtered + small[9:10] * own)).astype(BF)
 
 
@@ -295,22 +297,23 @@
             ),
             name="product_spectrum",
         )(products[number], halos[number], forward)
-        mixed = pl.pallas_call(
-            functools.partial(filter_kernel, blocks),
-            in_specs=[smem] + [vmem] * (12 + len(blocks)),
-            out_specs=vmem,
-            out_shape=jax.ShapeDtypeStruct((rows, width), BF),
-            scratch_shapes=[
-                pltpu.VMEM((8 * len(blocks), 128, 128), BF),
-                pltpu.VMEM((256, width), F32),
-            ],
-            compiler_params=params,
-            name="filter_and_gate",
-        )(
-            flags, query_rows, edge, along_z, products[number], spectrum,
-            *[priors[x] for x in blocks], *all_taps, forward, inverse,
-        )
-        handed.append(shift_by_one(mixed, "section", n_section))
+        for part in [blocks] if number == 0 else [(x,) for x in blocks]:
+            mixed = pl.pallas_call(
+                functools.partial(filter_kernel, part, 1024 * (part[0] - blocks[0])),
+                in_specs=[smem] + [vmem] * (12 + len(part)),
+                out_specs=vmem,
+                out_shape=jax.ShapeDtypeStruct((rows, 1024 * len(part)), BF),
+                scratch_shapes=[
+                    pltpu.VMEM((8 * len(part), 128, 128), BF),
+                    pltpu.VMEM((256, 1024 * len(part)), F32),
+                ],
+                compiler_params=params,
+                name="filter_and_gate",
+            )(
+                flags, query_rows, edge, along_z, products[number], spectrum,
+                *[priors[x] for x in part], *all_taps, forward, inverse,
+            )
+            handed.append(shift_by_one(mixed, "section", n_section))
     return jnp.concatenate(handed, axis=1)
 
 

time: 92.7 us -> 92.7 us (level)
  waiting for transfers between devices: 34.5 us -> 33.5 us
    ppermute x2 -> x3, waiting for transfers between devices: 10.6 us -> 9.68 us  [shift_by_one(): lax.ppermute(value, axes, [(i, (i + 1) % count) for i in range(count)])]
    pallas_call x2 -> x3, Pallas kernels: 6.49 us -> 7.42 us  [body(): pl.pallas_call(functools.partial(filter_kernel, part, 1024 * (part[0] - b...]
  transfers between devices with their start and end apart: 13 -> 14, of which waited for: 8 -> 8; matrix products, arithmetic and copies ran while one was open for 0% -> 0% of each run, Pallas kernels for 10% -> 11%
where the time goes in v4:
time: 92.7 us; the launch traced here: 92.2 us
  starting transfers between devices  34.1 us (37%)
  waiting for transfers between devices  33.5 us (36%)
  Pallas kernels  13.8 us (15%)
  blocking collectives  9.46 us (10%)
  other arithmetic  1.12 us (1%)
    ppermute x10, starting transfers between devices, send(): return lax.ppermute(value, ctx, pairs)  22.9 us
    ppermute x10, waiting for transfers between devices, send(): return lax.ppermute(value, ctx, pairs)  20.2 us
    all_to_all x1, starting transfers between devices, exchange(): return lax.all_to_all(copies, axis, split_axis=0, concat_axis=0, tiled=True)  10.3 us
    ppermute x3, waiting for transfers between devices, shift_by_one(): lax.ppermute(value, axes, [(i, (i + 1) % count) for i in range(count)])  9.68 us
    all_to_all x1, blocking collectives, exchange(): return lax.all_to_all(copies, axis, split_axis=0, concat_axis=0, tiled=True)  9.46 us
    pallas_call x3, Pallas kernels, body(): pl.pallas_call(functools.partial(filter_kernel, part, 1024 * (part[0] - b...  7.42 us
    all_to_all x1, waiting for transfers between devices, exchange(): return lax.all_to_all(copies, axis, split_axis=0, concat_axis=0, tiled=True)  3.63 us
    pallas_call x2, Pallas kernels, body(): pl.pallas_call(functools.partial(product_kernel, blocks), in_specs=[smem]...  2.87 us
  transfers between devices with their start and end apart: 14, of which 8 were waited for; matrix products, arithmetic and copies ran while one was open for 0% of the time, Pallas kernels for 11%

profile of v4, /device:TPU:32, one launch (start us, length us, event | category | flops | bytes accessed | tf_op | source)
XLA Modules:
  0.0 92.2 jit_solution(7662038831169479915)
XLA Ops:
  0.0 1.2 %prepare.1 = (bf16[8,4096]{1,0:T(8,128)(2,1)S(1)}, bf16[4,16,128]{2,1,0:T(8,128)(2,1)S(1)}, bf16[1,128,128]{2,1,0:T(8,128)(2,1)S(1)}) custom-call(bf16[128,4096]{1,0:T(8,128)(2,1)} %query_ref.7, bf16[128,4096]{1,0:T(8,128)(2,1)} %key_ref.5, bf16[128,4096]{1,0:T(8,128)(2,1)} %value_ref.5, bf16[1,3,3,128]{3,2,1,0:T(4,128)(2,1)} %short_ref.1, ...), custom_call_target="tpu_custom_call" | custom-call | tf_op jit(solution)/shard_map/prepare/pallas_call | solution.py:206
  1.2 9.5 %all_to_all.10.small_ref = bf16[4,16,128]{2,1,0:T(8,128)(2,1)S(1)} all-to-all(bf16[4,16,128]{2,1,0:T(8,128)(2,1)S(1)} %get-tuple-element.16), channel_id=1, replica_groups=mesh['section'=16,'ctx_x'=4,'ctx_z'=8] {'ctx_x'}, dimensions={0} | all-to-all | bytes 32768 | tf_op jit(solution)/shard_map/all_to_all | solution.py:181
  10.6 0.9 spread.1
  11.5 10.3 %all-to-all-start.1 = ((bf16[8,320,128]{2,1,0:T(8,128)(2,1)}), bf16[8,320,128]{2,1,0:T(8,128)(2,1)S(1)}, u32[]{:S(2)}, u32[]{:S(2)}) async-start(bf16[8,320,128]{2,1,0:T(8,128)(2,1)} %spread.1), calls=%async_computation.1 | async-start | bytes 1310720 | tf_op jit(solution)/shard_map/all_to_all | solution.py:181
  21.9 3.9 %collective-permute-start = (bf16[8,4096]{1,0:T(8,128)(2,1)S(1)}, bf16[8,4096]{1,0:T(8,128)(2,1)S(1)}, u32[]{:S(2)}, u32[]{:S(2)}) collective-permute-start(bf16[8,4096]{1,0:T(8,128)(2,1)S(1)} %get-tuple-element.18), channel_id=1, source_target_pairs={{0,1},{1,2},{2,3},{3,4},{4,5},{5,6},{6,7},{7,8},{8,9},{9,10},{10,1... | collective-permute-start | bytes 196616 | tf_op jit(solution)/shard_map/ppermute | solution.py:228
  25.8 0.1 pad_add_fusion.flags_ref
  25.9 12.0 %collective-permute-done.edge_ref = bf16[8,4096]{1,0:T(8,128)(2,1)S(1)} collective-permute-done((bf16[8,4096]{1,0:T(8,128)(2,1)S(1)}, bf16[8,4096]{1,0:T(8,128)(2,1)S(1)}, u32[]{:S(2)}, u32[]{:S(2)}) %collective-permute-start) | collective-permute-done | bytes 65568 | tf_op jit(solution)/shard_map/ppermute | solution.py:228
  37.8 3.6 %all-to-all-done.1.small_ref = bf16[8,320,128]{2,1,0:T(8,128)(2,1)S(1)} async-done(((bf16[8,320,128]{2,1,0:T(8,128)(2,1)}), bf16[8,320,128]{2,1,0:T(8,128)(2,1)S(1)}, u32[]{:S(2)}, u32[]{:S(2)}) %all-to-all-start.1) | async-done | bytes 655392 | tf_op jit(solution)/shard_map/all_to_all | solution.py:181
  41.5 1.4 %gated_product.2.own_ref = bf16[128,2048]{1,0:T(8,128)(2,1)S(1)} custom-call(s32[2]{0:T(128)S(1)} %pad_add_fusion.flags_ref, bf16[128,4096]{1,0:T(8,128)(2,1)S(1)} %copy-done.1, bf16[128,4096]{1,0:T(8,128)(2,1)S(1)} %copy-done.2, bf16[8,4096]{1,0:T(8,128)(2,1)S(1)} %collective-permute-done.edge_ref, bf16[8,320,128]{2,1,0:T(8,128)(2,1)S(1)} %all-to-all-done.1.small_ref), custom_call_target="tpu_custom_call" | custom-call | tf_op jit(solution)/shard_map/gated_product/pallas_call | solution.py:251
  42.9 2.1 %collective-permute-start.1 = (bf16[128,2048]{1,0:T(8,128)(2,1)S(1)}, bf16[128,2048]{1,0:T(8,128)(2,1)S(1)}, u32[]{:S(2)}, u32[]{:S(2)}) collective-permute-start(bf16[128,2048]{1,0:T(8,128)(2,1)S(1)} %gated_product.2.own_ref), channel_id=1, source_target_pairs={{0,1},{1,2},{2,3},{3,4},{4,5},{5,6},{6,7},{7,8},{8,9},{9,10},{10,1... | collective-permute-start | bytes 1572872 | tf_op jit(solution)/shard_map/ppermute | solution.py:228
  45.0 1.4 %gated_product.3.own_ref = bf16[128,2048]{1,0:T(8,128)(2,1)S(1)} custom-call(s32[2]{0:T(128)S(1)} %pad_add_fusion.flags_ref, bf16[128,4096]{1,0:T(8,128)(2,1)S(1)} %copy-done.1, bf16[128,4096]{1,0:T(8,128)(2,1)S(1)} %copy-done.2, bf16[8,4096]{1,0:T(8,128)(2,1)S(1)} %collective-permute-done.edge_ref, bf16[8,320,128]{2,1,0:T(8,128)(2,1)S(1)} %all-to-all-done.1.small_ref), custom_call_target="tpu_custom_call" | custom-call | tf_op jit(solution)/shard_map/gated_product/pallas_call | solution.py:251
  46.5 3.1 %collective-permute-start.2 = (bf16[8,128,128]{2,1,0:T(8,128)(2,1)S(1)}, bf16[8,128,128]{2,1,0:T(8,128)(2,1)S(1)}, u32[]{:S(2)}, u32[]{:S(2)}) collective-permute-start(bf16[8,128,128]{2,1,0:T(8,128)(2,1)S(1)} %get-tuple-element.27.refs_2_.refs_1_), channel_id=1, source_target_pairs={{0,24},{1,25},{2,26},{3,27},{4,28},{5,29},{6,30},{7,31},{8,0},{9,1... | collective-permute-start | bytes 786440 | tf_op jit(solution)/shard_map/ppermute | solution.py:228
  49.6 0.7 collective-permute-start.3
  50.3 1.4 %collective-permute-start.4 = (bf16[8,128,128]{2,1,0:T(8,128)(2,1)S(1)}, bf16[8,128,128]{2,1,0:T(8,128)(2,1)S(1)}, u32[]{:S(2)}, u32[]{:S(2)}) collective-permute-start(bf16[8,128,128]{2,1,0:T(8,128)(2,1)S(1)} %get-tuple-element.28.refs_0_), channel_id=1, source_target_pairs={{8,0},{16,8},{40,32},{48,40},{72,64},{80,72},{104,96},{112,104},{1... | collective-permute-start | bytes 786440 | tf_op jit(solution)/shard_map/ppermute | solution.py:228
  51.7 3.6 %collective-permute-start.8 = (bf16[128,2048]{1,0:T(8,128)(2,1)S(1)}, bf16[128,2048]{1,0:T(8,128)(2,1)S(1)}, u32[]{:S(2)}, u32[]{:S(2)}) collective-permute-start(bf16[128,2048]{1,0:T(8,128)(2,1)S(1)} %gated_product.3.own_ref), channel_id=1, source_target_pairs={{0,1},{1,2},{2,3},{3,4},{4,5},{5,6},{6,7},{7,8},{8,9},{9,10},{10,1... | collective-permute-start | bytes 1572872 | tf_op jit(solution)/shard_map/ppermute | solution.py:228
  55.3 1.8 %collective-permute-done.2.refs_3_.refs_2_ = bf16[8,128,128]{2,1,0:T(8,128)(2,1)S(1)} collective-permute-done((bf16[8,128,128]{2,1,0:T(8,128)(2,1)S(1)}, bf16[8,128,128]{2,1,0:T(8,128)(2,1)S(1)}, u32[]{:S(2)}, u32[]{:S(2)}) %collective-permute-start.2) | collective-permute-done | bytes 262176 | tf_op jit(solution)/shard_map/ppermute | solution.py:228
  57.1 1.3 %collective-permute-start.11 = (bf16[8,128,128]{2,1,0:T(8,128)(2,1)S(1)}, bf16[8,128,128]{2,1,0:T(8,128)(2,1)S(1)}, u32[]{:S(2)}, u32[]{:S(2)}) collective-permute-start(bf16[8,128,128]{2,1,0:T(8,128)(2,1)S(1)} %get-tuple-element.28.refs_0_), channel_id=1, source_target_pairs={{24,0},{56,32},{88,64},{120,96},{152,128},{184,160},{216,192},{248... | collective-permute-start | bytes 786440 | tf_op jit(solution)/shard_map/ppermute | solution.py:228
  58.4 1.5 %collective-permute-done.4.refs_1_ = bf16[8,128,128]{2,1,0:T(8,128)(2,1)S(1)} collective-permute-done((bf16[8,128,128]{2,1,0:T(8,128)(2,1)S(1)}, bf16[8,128,128]{2,1,0:T(8,128)(2,1)S(1)}, u32[]{:S(2)}, u32[]{:S(2)}) %collective-permute-start.4) | collective-permute-done | bytes 262176 | tf_op jit(solution)/shard_map/ppermute | solution.py:228
  59.9 4.3 %collective-permute-start.5 = (bf16[8,128,128]{2,1,0:T(8,128)(2,1)S(1)}, bf16[8,128,128]{2,1,0:T(8,128)(2,1)S(1)}, u32[]{:S(2)}, u32[]{:S(2)}) collective-permute-start(bf16[8,128,128]{2,1,0:T(8,128)(2,1)S(1)} %collective-permute-done.2.refs_3_.refs_2_), channel_id=1, source_target_pairs={{0,24},{1,25},{2,26},{3,27},{4,28},{5,29},{6,30},{7,31},{8,0},{9,1... | collective-permute-start | bytes 786440 | tf_op jit(solution)/shard_map/ppermute | solution.py:228
  64.2 1.3 %collective-permute-start.6 = (bf16[8,128,128]{2,1,0:T(8,128)(2,1)S(1)}, bf16[8,128,128]{2,1,0:T(8,128)(2,1)S(1)}, u32[]{:S(2)}, u32[]{:S(2)}) collective-permute-start(bf16[8,128,128]{2,1,0:T(8,128)(2,1)S(1)} %collective-permute-done.3.refs_5_.refs_4_), channel_id=1, source_target_pairs={{1,0},{9,8},{17,16},{25,24},{33,32},{41,40},{49,48},{57,56},{65,64... | collective-permute-start | bytes 786440 | tf_op jit(solution)/shard_map/ppermute | solution.py:228
  65.5 1.3 %collective-permute-start.9 = (bf16[8,128,128]{2,1,0:T(8,128)(2,1)S(1)}, bf16[8,128,128]{2,1,0:T(8,128)(2,1)S(1)}, u32[]{:S(2)}, u32[]{:S(2)}) collective-permute-start(bf16[8,128,128]{2,1,0:T(8,128)(2,1)S(1)} %collective-permute-done.4.refs_1_), channel_id=1, source_target_pairs={{8,0},{40,32},{72,64},{104,96},{136,128},{168,160},{200,192},{232,... | collective-permute-start | bytes 786440 | tf_op jit(solution)/shard_map/ppermute | solution.py:228
  66.8 0.7 product_spectrum.2.spec_ref
  67.5 2.6 %collective-permute-done.5.refs_4_.refs_3_ = bf16[8,128,128]{2,1,0:T(8,128)(2,1)S(1)} collective-permute-done((bf16[8,128,128]{2,1,0:T(8,128)(2,1)S(1)}, bf16[8,128,128]{2,1,0:T(8,128)(2,1)S(1)}, u32[]{:S(2)}, u32[]{:S(2)}) %collective-permute-start.5) | collective-permute-done | bytes 262176 | tf_op jit(solution)/shard_map/ppermute | solution.py:228
  70.1 2.3 %collective-permute-done.6.refs_6_.refs_5_ = bf16[8,128,128]{2,1,0:T(8,128)(2,1)S(1)} collective-permute-done((bf16[8,128,128]{2,1,0:T(8,128)(2,1)S(1)}, bf16[8,128,128]{2,1,0:T(8,128)(2,1)S(1)}, u32[]{:S(2)}, u32[]{:S(2)}) %collective-permute-start.6) | collective-permute-done | bytes 262176 | tf_op jit(solution)/shard_map/ppermute | solution.py:228
  72.5 3.2 %filter_and_gate.3 = bf16[128,2048]{1,0:T(8,128)(2,1)S(1)} custom-call(s32[2]{0:T(128)S(1)} %pad_add_fusion.flags_ref, bf16[128,4096]{1,0:T(8,128)(2,1)S(1)} %copy-done, bf16[8,4096]{1,0:T(8,128)(2,1)S(1)} %collective-permute-done.edge_ref, bf16[8,320,128]{2,1,0:T(8,128)(2,1)S(1)} %all-to-all-done.1.small_ref, bf16[128,2048]{1,0:T(8,128)(2,1)S(1)} %gated_product.2.own_ref, ...), custom_call_target="tpu_custom_call" | custom-call | tf_op jit(solution)/shard_map/filter_and_gate/pallas_call | solution.py:301
  75.7 0.7 product_spectrum.3.spec_ref
  76.5 2.1 %filter_and_gate.4 = bf16[128,1024]{1,0:T(8,128)(2,1)S(1)} custom-call(s32[2]{0:T(128)S(1)} %pad_add_fusion.flags_ref, bf16[128,4096]{1,0:T(8,128)(2,1)S(1)} %copy-done, bf16[8,4096]{1,0:T(8,128)(2,1)S(1)} %collective-permute-done.edge_ref, bf16[8,320,128]{2,1,0:T(8,128)(2,1)S(1)} %all-to-all-done.1.small_ref, bf16[128,2048]{1,0:T(8,128)(2,1)S(1)} %gated_product.3.own_ref, ...), custom_call_target="tpu_custom_call" | custom-call | tf_op jit(solution)/shard_map/filter_and_gate/pallas_call | solution.py:301
  78.6 0.8 collective-permute-start.10
  79.3 2.1 %filter_and_gate.5 = bf16[128,1024]{1,0:T(8,128)(2,1)S(1)} custom-call(s32[2]{0:T(128)S(1)} %pad_add_fusion.flags_ref, bf16[128,4096]{1,0:T(8,128)(2,1)S(1)} %copy-done, bf16[8,4096]{1,0:T(8,128)(2,1)S(1)} %collective-permute-done.edge_ref, bf16[8,320,128]{2,1,0:T(8,128)(2,1)S(1)} %all-to-all-done.1.small_ref, bf16[128,2048]{1,0:T(8,128)(2,1)S(1)} %gated_product.3.own_ref, ...), custom_call_target="tpu_custom_call" | custom-call | tf_op jit(solution)/shard_map/filter_and_gate/pallas_call | solution.py:301
  81.5 6.9 %collective-permute-done.10 = bf16[128,1024]{1,0:T(8,128)(2,1)S(1)} collective-permute-done((bf16[128,1024]{1,0:T(8,128)(2,1)S(1)}, bf16[128,1024]{1,0:T(8,128)(2,1)S(1)}, u32[]{:S(2)}, u32[]{:S(2)}) %collective-permute-start.10) | collective-permute-done | bytes 262176 | tf_op jit(solution)/shard_map/ppermute | solution.py:177
  88.3 2.8 %collective-permute-done.12 = bf16[128,1024]{1,0:T(8,128)(2,1)S(1)} collective-permute-done((bf16[128,1024]{1,0:T(8,128)(2,1)S(1)}, bf16[128,1024]{1,0:T(8,128)(2,1)S(1)}, u32[]{:S(2)}, u32[]{:S(2)}) %collective-permute-start.12) | collective-permute-done | bytes 262176 | tf_op jit(solution)/shard_map/ppermute | solution.py:177
  91.2 1.0 %pad_maximum_fusion = bf16[128,4096]{1,0:T(8,128)(2,1)} fusion(bf16[128,1024]{1,0:T(8,128)(2,1)S(1)} %collective-permute-done.12, bf16[128,1024]{1,0:T(8,128)(2,1)S(1)} %collective-permute-done.10, bf16[128,2048]{1,0:T(8,128)(2,1)S(1)} %collective-permute-done.7), kind=kLoop, calls=%fused_computation | loop fusion | flops 3145728 | bytes 2097152 | tf_op jit(solution)/shard_map/concatenate | solution.py:317
  (21 shorter events, 0.1 us)
Async XLA Ops:
  0.0 41.5 %copy-start.1 = (bf16[128,4096]{1,0:T(8,128)(2,1)S(1)}, bf16[128,4096]{1,0:T(8,128)(2,1)}, u32[]{:S(2)}) copy-start(bf16[128,4096]{1,0:T(8,128)(2,1)} %key_ref.5) | copy-start | bytes 3145732
  0.0 41.5 %copy-start.2 = (bf16[128,4096]{1,0:T(8,128)(2,1)S(1)}, bf16[128,4096]{1,0:T(8,128)(2,1)}, u32[]{:S(2)}) copy-start(bf16[128,4096]{1,0:T(8,128)(2,1)} %value_ref.5) | copy-start | bytes 3145732
  0.0 10.6 %copy-start.5 = (bf16[1,128,128]{2,1,0:T(8,128)(2,1)S(1)}, bf16[1,128,128]{2,1,0:T(8,128)(2,1)}, u32[]{:S(2)}) copy-start(bf16[1,128,128]{2,1,0:T(8,128)(2,1)} %taps_ref.1) | copy-start | bytes 98308
  11.5 29.9 %all-to-all-start.1 = ((bf16[8,320,128]{2,1,0:T(8,128)(2,1)}), bf16[8,320,128]{2,1,0:T(8,128)(2,1)S(1)}, u32[]{:S(2)}, u32[]{:S(2)}) async-start(bf16[8,320,128]{2,1,0:T(8,128)(2,1)} %spread.1), calls=%async_computation.1 | async-start | bytes 1310720 | tf_op jit(solution)/shard_map/all_to_all | solution.py:181
  21.9 16.0 %collective-permute-start = (bf16[8,4096]{1,0:T(8,128)(2,1)S(1)}, bf16[8,4096]{1,0:T(8,128)(2,1)S(1)}, u32[]{:S(2)}, u32[]{:S(2)}) collective-permute-start(bf16[8,4096]{1,0:T(8,128)(2,1)S(1)} %get-tuple-element.18), channel_id=1, source_target_pairs={{0,1},{1,2},{2,3},{3,4},{4,5},{5,6},{6,7},{7,8},{8,9},{9,10},{10,1... | collective-permute-start | bytes 196616 | tf_op jit(solution)/shard_map/ppermute | solution.py:228
  42.9 23.9 %copy-start.3 = (bf16[512,256]{1,0:T(8,128)(2,1)S(1)}, bf16[512,256]{1,0:T(8,128)(2,1)}, u32[]{:S(2)}) copy-start(bf16[512,256]{1,0:T(8,128)(2,1)} %constant.14.clone.forward_ref.refs_7_.refs_6_) | copy-start | bytes 786436
  42.9 22.5 %collective-permute-start.1 = (bf16[128,2048]{1,0:T(8,128)(2,1)S(1)}, bf16[128,2048]{1,0:T(8,128)(2,1)S(1)}, u32[]{:S(2)}, u32[]{:S(2)}) collective-permute-start(bf16[128,2048]{1,0:T(8,128)(2,1)S(1)} %gated_product.2.own_ref), channel_id=1, source_target_pairs={{0,1},{1,2},{2,3},{3,4},{4,5},{5,6},{6,7},{7,8},{8,9},{9,10},{10,1... | collective-permute-start | bytes 1572872 | tf_op jit(solution)/shard_map/ppermute | solution.py:228
  46.5 10.6 %collective-permute-start.2 = (bf16[8,128,128]{2,1,0:T(8,128)(2,1)S(1)}, bf16[8,128,128]{2,1,0:T(8,128)(2,1)S(1)}, u32[]{:S(2)}, u32[]{:S(2)}) collective-permute-start(bf16[8,128,128]{2,1,0:T(8,128)(2,1)S(1)} %get-tuple-element.27.refs_2_.refs_1_), channel_id=1, source_target_pairs={{0,24},{1,25},{2,26},{3,27},{4,28},{5,29},{6,30},{7,31},{8,0},{9,1... | collective-permute-start | bytes 786440 | tf_op jit(solution)/shard_map/ppermute | solution.py:228
  49.6 8.8 %collective-permute-start.3 = (bf16[8,128,128]{2,1,0:T(8,128)(2,1)S(1)}, bf16[8,128,128]{2,1,0:T(8,128)(2,1)S(1)}, u32[]{:S(2)}, u32[]{:S(2)}) collective-permute-start(bf16[8,128,128]{2,1,0:T(8,128)(2,1)S(1)} %get-tuple-element.27.refs_2_.refs_1_), channel_id=1, source_target_pairs={{1,9},{2,10},{3,11},{4,12},{5,13},{6,14},{7,15},{9,17},{10,18},{11... | collective-permute-start | bytes 786440 | tf_op jit(solution)/shard_map/ppermute | solution.py:228
  50.3 22.2 %copy-start = (bf16[128,4096]{1,0:T(8,128)(2,1)S(1)}, bf16[128,4096]{1,0:T(8,128)(2,1)}, u32[]{:S(2)}) copy-start(bf16[128,4096]{1,0:T(8,128)(2,1)} %query_ref.7) | copy-start | bytes 3145732
  50.3 22.2 %copy-start.4 = (bf16[256,256]{1,0:T(8,128)(2,1)S(1)}, bf16[256,256]{1,0:T(8,128)(2,1)}, u32[]{:S(2)}) copy-start(bf16[256,256]{1,0:T(8,128)(2,1)} %constant.15.clone.refs_8_.refs_7_) | copy-start | bytes 393220
  50.3 9.6 %collective-permute-start.4 = (bf16[8,128,128]{2,1,0:T(8,128)(2,1)S(1)}, bf16[8,128,128]{2,1,0:T(8,128)(2,1)S(1)}, u32[]{:S(2)}, u32[]{:S(2)}) collective-permute-start(bf16[8,128,128]{2,1,0:T(8,128)(2,1)S(1)} %get-tuple-element.28.refs_0_), channel_id=1, source_target_pairs={{8,0},{16,8},{40,32},{48,40},{72,64},{80,72},{104,96},{112,104},{1... | collective-permute-start | bytes 786440 | tf_op jit(solution)/shard_map/ppermute | solution.py:228
  51.7 24.0 %collective-permute-start.8 = (bf16[128,2048]{1,0:T(8,128)(2,1)S(1)}, bf16[128,2048]{1,0:T(8,128)(2,1)S(1)}, u32[]{:S(2)}, u32[]{:S(2)}) collective-permute-start(bf16[128,2048]{1,0:T(8,128)(2,1)S(1)} %gated_product.3.own_ref), channel_id=1, source_target_pairs={{0,1},{1,2},{2,3},{3,4},{4,5},{5,6},{6,7},{7,8},{8,9},{9,10},{10,1... | collective-permute-start | bytes 1572872 | tf_op jit(solution)/shard_map/ppermute | solution.py:228
  57.1 22.2 %collective-permute-start.11 = (bf16[8,128,128]{2,1,0:T(8,128)(2,1)S(1)}, bf16[8,128,128]{2,1,0:T(8,128)(2,1)S(1)}, u32[]{:S(2)}, u32[]{:S(2)}) collective-permute-start(bf16[8,128,128]{2,1,0:T(8,128)(2,1)S(1)} %get-tuple-element.28.refs_0_), channel_id=1, source_target_pairs={{24,0},{56,32},{88,64},{120,96},{152,128},{184,160},{216,192},{248... | collective-permute-start | bytes 786440 | tf_op jit(solution)/shard_map/ppermute | solution.py:228
  59.9 10.2 %collective-permute-start.5 = (bf16[8,128,128]{2,1,0:T(8,128)(2,1)S(1)}, bf16[8,128,128]{2,1,0:T(8,128)(2,1)S(1)}, u32[]{:S(2)}, u32[]{:S(2)}) collective-permute-start(bf16[8,128,128]{2,1,0:T(8,128)(2,1)S(1)} %collective-permute-done.2.refs_3_.refs_2_), channel_id=1, source_target_pairs={{0,24},{1,25},{2,26},{3,27},{4,28},{5,29},{6,30},{7,31},{8,0},{9,1... | collective-permute-start | bytes 786440 | tf_op jit(solution)/shard_map/ppermute | solution.py:228
  64.2 8.3 %collective-permute-start.6 = (bf16[8,128,128]{2,1,0:T(8,128)(2,1)S(1)}, bf16[8,128,128]{2,1,0:T(8,128)(2,1)S(1)}, u32[]{:S(2)}, u32[]{:S(2)}) collective-permute-start(bf16[8,128,128]{2,1,0:T(8,128)(2,1)S(1)} %collective-permute-done.3.refs_5_.refs_4_), channel_id=1, source_target_pairs={{1,0},{9,8},{17,16},{25,24},{33,32},{41,40},{49,48},{57,56},{65,64... | collective-permute-start | bytes 786440 | tf_op jit(solution)/shard_map/ppermute | solution.py:228
  65.5 11.0 %collective-permute-start.9 = (bf16[8,128,128]{2,1,0:T(8,128)(2,1)S(1)}, bf16[8,128,128]{2,1,0:T(8,128)(2,1)S(1)}, u32[]{:S(2)}, u32[]{:S(2)}) collective-permute-start(bf16[8,128,128]{2,1,0:T(8,128)(2,1)S(1)} %collective-permute-done.4.refs_1_), channel_id=1, source_target_pairs={{8,0},{40,32},{72,64},{104,96},{136,128},{168,160},{200,192},{232,... | collective-permute-start | bytes 786440 | tf_op jit(solution)/shard_map/ppermute | solution.py:228
  75.7 15.4 %collective-permute-start.7 = (bf16[128,2048]{1,0:T(8,128)(2,1)S(1)}, bf16[128,2048]{1,0:T(8,128)(2,1)S(1)}, u32[]{:S(2)}, u32[]{:S(2)}) collective-permute-start(bf16[128,2048]{1,0:T(8,128)(2,1)S(1)} %filter_and_gate.3), channel_id=1, source_target_pairs={{0,32},{32,64},{64,96},{96,128},{128,160},{160,192},{192,224},{224... | collective-permute-start | bytes 1572872 | tf_op jit(solution)/shard_map/ppermute | solution.py:177
  78.6 9.8 %collective-permute-start.10 = (bf16[128,1024]{1,0:T(8,128)(2,1)S(1)}, bf16[128,1024]{1,0:T(8,128)(2,1)S(1)}, u32[]{:S(2)}, u32[]{:S(2)}) collective-permute-start(bf16[128,1024]{1,0:T(8,128)(2,1)S(1)} %filter_and_gate.4), channel_id=1, source_target_pairs={{0,32},{32,64},{64,96},{96,128},{128,160},{160,192},{192,224},{224... | collective-permute-start | bytes 786440 | tf_op jit(solution)/shard_map/ppermute | solution.py:177
  81.4 9.7 %collective-permute-start.12 = (bf16[128,1024]{1,0:T(8,128)(2,1)S(1)}, bf16[128,1024]{1,0:T(8,128)(2,1)S(1)}, u32[]{:S(2)}, u32[]{:S(2)}) collective-permute-start(bf16[128,1024]{1,0:T(8,128)(2,1)S(1)} %filter_and_gate.5), channel_id=1, source_target_pairs={{0,32},{32,64},{64,96},{96,128},{128,160},{160,192},{192,224},{224... | collective-permute-start | bytes 786440 | tf_op jit(solution)/shard_map/ppermute | solution.py:177
